TPU v7x, 32 devices: a whole 2x2x4 slice. The times are simulated.
32 devices in a mesh: grp: 4 (over y, core), shard: 8 (over z, x).
Axes of the slice: x: 2, y: 2, z: 4, core: 2. Of those that a mesh axis runs over, the one named last changes fastest.
Arguments:
- events: bfloat16 [4096, 1024], P(('grp', 'shard')), may hold values from -6 to 6
- user_ids: int32 [4096], P(('grp', 'shard')), may hold values from 0 to 31, as said below
- session_break: int32 [4096], P(('grp', 'shard')), may hold values 0 or 1
- in_gain: float32 [1024], replicated, may hold values from 0.1 to 1.9
- in_weight: bfloat16 [1024, 2048], replicated, may hold values from -0.1875 to 0.1875
- decay_rates: float32 [1024], replicated, may hold values from 0.0001 to 0.04
- keep_factor: float32 [1024], replicated, may hold values from 0.4 to 0.8
- out_gain: float32 [1024], replicated, may hold values from 0.1 to 1.9
- out_weight: bfloat16 [1024, 1024], replicated, may hold values from -0.1875 to 0.1875
Outputs:
- mixed: bfloat16 [4096, 1024], P(('grp', 'shard'))
Inputs may be any that keep to these rules, and one draw needn't show every extreme that they name: The owner range of an event is user_ids // 4. In every aligned block of 128 rows at most 34 rows share an owner range; in every aligned stretch of 1024 rows one owner range has exactly 34 rows in each of its blocks.
All inputs are finite; a program needn't handle non-finite values. No bound on the sum of `session_break` on one device may be relied on, other than what follows from the above.
Results may differ from a plain program's by a relative error of at most 0.0057.
Values may be sent and summed in bfloat16 or wider, within the bound.
No kernel may reach another device: no remote copies, remote signals or barrier semaphores. Data moves between devices by JAX's collectives and lax.ppermute only.
A program may use at most 64 MiB of HBM per device.

v0:
```python
import jax
import jax.numpy as jnp
from jax import lax
from jax.sharding import PartitionSpec as P

U_DEV = 4


def carried_in(shard, axis, combine, identity):
    length, index = (lax.axis_size(axis), lax.axis_index(axis))
    everything = jax.tree.map(lambda part: lax.all_gather(part, axis), shard)
    start = jax.tree.map(
        lambda part, zero: jnp.broadcast_to(jnp.asarray(zero, part.dtype), part.shape),
        shard,
        identity,
    )

    def lap(k, before):
        reached = k < index
        new = combine(before, jax.tree.map(lambda part: part[k], everything))
        return jax.tree.map(lambda a, b: jnp.where(reached, a, b), new, before)

    return lax.fori_loop(0, length, lap, start)


def rms_scale(values, gain_vec):
    return values * lax.rsqrt(jnp.mean(values * values, axis=-1, keepdims=True) + 1e-06) * gain_vec


def project(source_rows, in_gain, in_weight):
    normed = rms_scale(source_rows.astype(jnp.float32), in_gain).astype(jnp.bfloat16)
    return jnp.dot(normed, in_weight, preferred_element_type=jnp.float32).astype(jnp.bfloat16)


def combine(earlier_pair, later_pair):
    return (earlier_pair[0] * later_pair[0], later_pair[0] * earlier_pair[1] + later_pair[1])


def mask_product(mask_rows, data_rows):
    return jnp.dot(mask_rows, data_rows, preferred_element_type=jnp.float32)


def exact_einsum(form, left, right):
    return jnp.einsum(form, left, right.astype(jnp.float32), precision=lax.Precision.HIGHEST)


def on_device(
    events,
    user_ids,
    session_break,
    in_gain,
    in_weight,
    decay_rates,
    keep_factor,
    out_gain,
    out_weight,
):
    owners = lax.axis_size("shard")
    local_rows, feature_width = events.shape
    capacity = 2 * local_rows // owners + 2
    slot_count = owners * capacity
    destination = user_ids // U_DEV
    onehot_dest = (destination[:, None] == jnp.arange(owners, dtype=jnp.int32)[None, :]).astype(
        jnp.bfloat16
    )
    row_index = jnp.arange(local_rows, dtype=jnp.int32)
    earlier = (row_index[:, None] > row_index[None, :]).astype(jnp.bfloat16)
    slot_rank = jnp.sum(
        mask_product(earlier, onehot_dest) * onehot_dest.astype(jnp.float32), axis=1
    ).astype(jnp.int32)
    slot_index = destination * capacity + slot_rank
    send_users = jnp.full((slot_count,), -1, jnp.int32).at[slot_index].set(user_ids % U_DEV)
    send_breaks = jnp.zeros((slot_count,), jnp.int32).at[slot_index].set(session_break)
    send_rows = jnp.zeros((slot_count, feature_width), jnp.bfloat16).at[slot_index].set(events)
    got_rows, got_users, got_breaks = (
        lax.all_to_all(send_rows, "shard", split_axis=0, concat_axis=0, tiled=True),
        lax.all_to_all(send_users, "shard", split_axis=0, concat_axis=0, tiled=True),
        lax.all_to_all(send_breaks, "shard", split_axis=0, concat_axis=0, tiled=True),
    )
    projected = project(got_rows, in_gain, in_weight)
    gate_part = projected[:, :feature_width].astype(jnp.float32)
    value_part = projected[:, feature_width:].astype(jnp.float32)
    member = (got_users[:, None] == jnp.arange(U_DEV, dtype=jnp.int32)[None, :]).astype(jnp.float32)
    valid_rows = jnp.sum(member, axis=1)
    tally_cols = jnp.stack([valid_rows, got_breaks.astype(jnp.float32) * valid_rows], axis=1)
    member_blocks = member.reshape(owners, capacity, U_DEV)
    tally_blocks = tally_cols.reshape(owners, capacity, 2)
    value_blocks = value_part.reshape(owners, capacity, feature_width)
    slot_pos = jnp.arange(capacity, dtype=jnp.int32)
    causal = (slot_pos[:, None] >= slot_pos[None, :]).astype(jnp.float32)
    within = exact_einsum("kiu,kju->kij", member_blocks, member_blocks) * causal[None, :, :]
    counts_pair = exact_einsum("kij,kjt->kit", within, tally_blocks)
    log_keep = jnp.log(keep_factor)
    log_level = -decay_rates * counts_pair[:, :, 0:1] + log_keep * counts_pair[:, :, 1:2]
    growth = jnp.exp(log_level)
    scaled = jnp.exp(-log_level) * value_blocks
    local_state = growth * exact_einsum("kij,kjd->kid", within, scaled)
    totals = exact_einsum("kiu,kit->kut", member_blocks, tally_blocks)
    piece_span = jnp.exp(-decay_rates * totals[:, :, 0:1] + log_keep * totals[:, :, 1:2])
    piece_ends = piece_span * exact_einsum("kiu,kid->kud", member_blocks, scaled)
    inclusive = lax.associative_scan(combine, (piece_span, piece_ends), axis=0)
    prefix_span = jnp.concatenate([jnp.ones_like(piece_span[:1]), inclusive[0][:-1]], axis=0)
    prefix_ends = jnp.concatenate([jnp.zeros_like(piece_ends[:1]), inclusive[1][:-1]], axis=0)
    block_span = inclusive[0][-1]
    block_ends = inclusive[1][-1]
    identity = (jnp.ones_like(block_span), jnp.zeros_like(block_ends))
    carry_start = carried_in((block_span, block_ends), "grp", combine, identity)[1]
    piece_start = prefix_span * carry_start[None, :, :] + prefix_ends
    hidden_blocks = local_state + growth * exact_einsum("kiu,kud->kid", member_blocks, piece_start)
    hidden = hidden_blocks.reshape(slot_count, feature_width)
    mixed_part = (rms_scale(hidden, out_gain) * jax.nn.silu(gate_part)).astype(jnp.bfloat16)
    back_rows = (
        got_rows.astype(jnp.float32)
        + jnp.dot(mixed_part, out_weight, preferred_element_type=jnp.float32)
    ).astype(jnp.bfloat16)
    returned = lax.all_to_all(back_rows, "shard", split_axis=0, concat_axis=0, tiled=True)[
        slot_index
    ]
    return returned


def solution(mesh):
    return jax.shard_map(
        on_device,
        mesh=mesh,
        in_specs=(
            P(("grp", "shard"), None),
            P(("grp", "shard")),
            P(("grp", "shard")),
            P(),
            P(),
            P(),
            P(),
            P(),
            P(),
        ),
        out_specs=P(("grp", "shard"), None),
        check_vma=False,
    )
```

profile of v0, /device:TPU:0, one launch (start us, length us, event | category | flops | bytes accessed | tf_op | source)
XLA Modules:
  0.0 139.8 jit_solution(11350926843758584566)
XLA Ops:
  0.0 0.8 and_select_fusion
  1.0 1.0 scatter_custom_fusion.1
  2.7 7.3 %all-to-all-start.1 = ((s32[8,34,1]{1,2,0:T(1,128)}), s32[8,34,1]{1,2,0:T(1,128)S(1)}, u32[]{:S(2)}, u32[]{:S(2)}) async-start(s32[8,34,1]{1,2,0:T(1,128)} %all_to_all.28), calls=%async_computation.1 | async-start | bytes 8192 | tf_op jit(solution)/shard_map/all_to_all | solution.py:77
  10.0 1.7 %scatter_custom_fusion = bf16[272,1024]{1,0:T(8,128)(2,1)S(1)} fusion(s32[128]{0:T(128)S(1)} %compare_select_fusion, bf16[128,1024]{1,0:T(8,128)(2,1)} %param.11, bf16[]{:T(256)} %constant.65.clone.1), kind=kCustom, calls=%fused_computation.44 | custom fusion | bytes 557568 | tf_op jit(solution)/shard_map/scatter | solution.py:74
  11.7 1.0 all_to_all.26
  12.7 1.1 scatter_custom_fusion.2
  14.6 1.8 %all-to-all-done.1 = s32[8,34,1]{1,2,0:T(1,128)S(1)} async-done(((s32[8,34,1]{1,2,0:T(1,128)}), s32[8,34,1]{1,2,0:T(1,128)S(1)}, u32[]{:S(2)}, u32[]{:S(2)}) %all-to-all-start.1) | async-done | bytes 1120 | tf_op jit(solution)/shard_map/all_to_all | solution.py:77
  16.4 4.2 %all-to-all-start.2 = ((s32[8,34,1]{1,2,0:T(1,128)}), s32[8,34,1]{1,2,0:T(1,128)S(1)}, u32[]{:S(2)}, u32[]{:S(2)}) async-start(s32[8,34,1]{1,2,0:T(1,128)} %all_to_all.30), calls=%async_computation.2 | async-start | bytes 8192 | tf_op jit(solution)/shard_map/all_to_all | solution.py:78
  22.0 5.1 %all-to-all-done.2 = s32[8,34,1]{1,2,0:T(1,128)S(1)} async-done(((s32[8,34,1]{1,2,0:T(1,128)}), s32[8,34,1]{1,2,0:T(1,128)S(1)}, u32[]{:S(2)}, u32[]{:S(2)}) %all-to-all-start.2) | async-done | bytes 1120 | tf_op jit(solution)/shard_map/all_to_all | solution.py:78
  27.1 3.5 %all-to-all-start = ((bf16[8,34,1024]{2,1,0:T(8,128)(2,1)}), bf16[8,34,1024]{2,1,0:T(8,128)(2,1)S(1)}, u32[]{:S(2)}, u32[]{:S(2)}) async-start(bf16[8,34,1024]{2,1,0:T(8,128)(2,1)} %all_to_all.26), calls=%async_computation | async-start | bytes 1310720 | tf_op jit(solution)/shard_map/all_to_all | solution.py:76
  33.1 13.0 %all-to-all-done = bf16[8,34,1024]{2,1,0:T(8,128)(2,1)S(1)} async-done(((bf16[8,34,1024]{2,1,0:T(8,128)(2,1)}), bf16[8,34,1024]{2,1,0:T(8,128)(2,1)S(1)}, u32[]{:S(2)}, u32[]{:S(2)}) %all-to-all-start) | async-done | bytes 557088 | tf_op jit(solution)/shard_map/all_to_all | solution.py:76
  46.5 1.2 reshape.93
  47.6 3.9 %convolution_convert_fusion = bf16[272,2048]{1,0:T(8,128)(2,1)S(1)} fusion(bf16[1024,2048]{1,0:T(8,128)(2,1)} %param.15, f32[272,1024]{1,0:T(8,128)} %reshape.93, f32[1024]{0:T(1024)S(1)} %copy-done.22, f32[272]{0:T(512)S(1)} %rsqrt.23), kind=kOutput, calls=%fused_computation.7 | convolution fusion | flops 1142243328 | bytes 6427712 | tf_op jit(solution)/shard_map/dot_general | solution.py:32
  51.6 1.0 copy-done.5
  52.7 1.2 reshape.95
  53.9 2.9 %fusion.9 = f32[8,34,1024]{2,1,0:T(8,128)S(1)} fusion(f32[8,34,34]{2,1,0:T(8,128)} %copy-done.2, f32[8,34,1024]{2,1,0:T(8,128)} %reshape.95, f32[8,34]{1,0:T(8,128)} %bitcast.32, f32[1024]{0:T(1024)} %copy-done.6, f32[8,34]{1,0:T(8,128)} %bitcast.29, f32[1024]{0:T(1024)} %copy-done.8), kind=kOutput, calls=%fused_computation.28 | convolution fusion | flops 115032064 | bytes 2275584 | tf_op jit(solution)/shard_map/kij,kjd->kid/dot_general | solution.py:44
  57.0 0.9 convolution_multiply_fusion.1
  59.8 2.0 %pad.43 = f32[4,4,1024]{2,1,0:T(4,128)} pad(f32[2,4,1024]{2,1,0:T(4,128)} %get-tuple-element.151, f32[]{:T(128)} %constant.72.clone.1), padding=1_0_1x0_0_0x0_0_0 | pad | bytes 98308 | tf_op jit(solution)/shard_map/pad | solution.py:101
  61.8 1.4 pad_maximum_fusion.2
  63.2 2.0 %pad.42 = f32[4,4,1024]{2,1,0:T(4,128)} pad(f32[2,4,1024]{2,1,0:T(4,128)} %get-tuple-element.152, f32[]{:T(128)} %constant.72.clone.1), padding=0_1_1x0_0_0x0_0_0 | pad | bytes 98308 | tf_op jit(solution)/shard_map/pad | solution.py:101
  65.1 2.0 %pad.49 = f32[4,4,1024]{2,1,0:T(4,128)} pad(f32[2,4,1024]{2,1,0:T(4,128)} %get-tuple-element.150, f32[]{:T(128)} %constant.72.clone.1), padding=1_0_1x0_0_0x0_0_0 | pad | bytes 98308 | tf_op jit(solution)/shard_map/pad | solution.py:101
  67.1 2.0 %pad.48 = f32[4,4,1024]{2,1,0:T(4,128)} pad(f32[2,4,1024]{2,1,0:T(4,128)} %get-tuple-element.153, f32[]{:T(128)} %constant.72.clone.1), padding=0_1_1x0_0_0x0_0_0 | pad | bytes 98308 | tf_op jit(solution)/shard_map/pad | solution.py:101
  69.1 1.5 %add.157 = f32[4,4,1024]{2,1,0:T(4,128)} add(f32[4,4,1024]{2,1,0:T(4,128)} %pad.48, f32[4,4,1024]{2,1,0:T(4,128)} %pad.49) | non-fusion elementwise | flops 16384 | bytes 196608 | tf_op jit(solution)/shard_map/add | solution.py:101
  70.6 1.6 %add_multiply_fusion.1 = (f32[3,4,1024]{2,1,0:T(4,128)}, f32[3,4,1024]{2,1,0:T(4,128)}) fusion(f32[4,4,1024]{2,1,0:T(4,128)} %pad.43, f32[4,4,1024]{2,1,0:T(4,128)} %pad.42, f32[8,4,1024]{2,1,0:T(4,128)S(1)} %add_exponential_fusion, f32[8,4,1024]{2,1,0:T(4,128)} %copy-done.4, f32[4,4,1024]{2,1,0:T(4,128)} %pad.49, f32[4,4,1024]{2,1,0:T(4,128)} %pad.48), kind=kLoop, calls=%fused_computation.60 | loop fusion | flops 61440 | bytes 393216 | tf_op jit(solution)/shard_map/mul | solution.py:36
  72.2 0.9 add.150
  73.1 1.9 %pad.45 = f32[8,4,1024]{2,1,0:T(4,128)} pad(f32[4,4,1024]{2,1,0:T(4,128)S(1)} %add.150, f32[]{:T(128)} %constant.72.clone.1), padding=1_0_1x0_0_0x0_0_0 | pad | bytes 196612 | tf_op jit(solution)/shard_map/pad | solution.py:101
  75.0 1.9 %pad.108 = f32[7,4,1024]{2,1,0:T(4,128)} pad(f32[4,4,1024]{2,1,0:T(4,128)S(1)} %add.150, f32[]{:T(128)} %constant.72.clone.1), padding=0_0_1x0_0_0x0_0_0 | pad | bytes 180228
  76.9 0.8 pad_maximum_fusion.1
  77.7 1.9 %pad.67 = f32[7,4,1024]{2,1,0:T(4,128)} pad(f32[4,4,1024]{2,1,0:T(4,128)S(1)} %pad_maximum_fusion.1, f32[]{:T(128)} %constant.72.clone.1), padding=0_0_1x0_0_0x0_0_0 | pad | bytes 180228 | tf_op jit(solution)/shard_map/slice | solution.py:103
  79.6 1.9 %pad.50 = f32[8,4,1024]{2,1,0:T(4,128)} pad(f32[4,4,1024]{2,1,0:T(4,128)S(1)} %pad_maximum_fusion.1, f32[]{:T(128)} %constant.72.clone.1), padding=0_1_1x0_0_0x0_0_0 | pad | bytes 196612 | tf_op jit(solution)/shard_map/pad | solution.py:101
  81.5 1.5 %pad.106 = f32[8,4,1024]{2,1,0:T(4,128)S(1)} pad(f32[4,4,1024]{2,1,0:T(4,128)} %add.157, f32[]{:T(128)} %constant.72.clone.1), padding=1_0_1x0_0_0x0_0_0 | pad | bytes 196612
  83.0 1.4 %pad_maximum_fusion = f32[4,4,1024]{2,1,0:T(4,128)} fusion(f32[3,4,1024]{2,1,0:T(4,128)} %get-tuple-element.128, f32[1,4,1024]{2,1,0:T(4,128)} %slice.151), kind=kLoop, calls=%fused_computation.52 | loop fusion | flops 16384 | bytes 131072 | tf_op jit(solution)/shard_map/concatenate | solution.py:101
  84.4 3.3 %pad.44 = f32[8,4,1024]{2,1,0:T(4,128)} pad(f32[4,4,1024]{2,1,0:T(4,128)} %pad_maximum_fusion, f32[]{:T(128)} %constant.72.clone.1), padding=0_1_1x0_0_0x0_0_0 | pad | bytes 196612 | tf_op jit(solution)/shard_map/pad | solution.py:101
  88.5 5.7 %all_gather.6 = f32[4,4,1024]{2,1,0:T(4,128)} all-gather(f32[1,4,1024]{2,1,0:T(4,128)S(1)} %slice.228), channel_id=1, replica_groups=mesh['grp'=4,'shard'=8] {'grp'}, dimensions={0}, use_global_device_ids=true | all-gather | bytes 81920 | tf_op jit(solution)/shard_map/all_gather | solution.py:11
  94.1 1.6 %slice_add_fusion.5 = f32[7,4,1024]{2,1,0:T(4,128)} fusion(f32[7,4,1024]{2,1,0:T(4,128)} %pad.67, f32[8,4,1024]{2,1,0:T(4,128)S(1)} %pad.106), kind=kLoop, calls=%fused_computation.117 | loop fusion | flops 28672 | bytes 344064 | tf_op jit(solution)/shard_map/add | solution.py:101
  96.4 5.2 %all_gather.7 = f32[4,4,1024]{2,1,0:T(4,128)S(1)} all-gather(f32[1,4,1024]{2,1,0:T(4,128)S(1)} %slice_add_fusion.3), channel_id=1, replica_groups=mesh['grp'=4,'shard'=8] {'grp'}, dimensions={0}, use_global_device_ids=true | all-gather | bytes 81920 | tf_op jit(solution)/shard_map/all_gather | solution.py:11
  101.6 3.0 %while.14 = (s32[]{:T(128)}, f32[4,1024]{1,0:T(4,128)S(1)}, s32[]{:T(128)}, f32[4,4,1024]{2,1,0:T(4,128)}, f32[4,4,1024]{2,1,0:T(4,128)S(1)}, /*index=5*/s32[]{:T(128)}, s32[]{:T(128)}) while((s32[]{:T(128)}, f32[4,1024]{1,0:T(4,128)S(1)}, s32[]{:T(128)}, f32[4,4,1024]{2,1,0:T(4,128)}, f32[4,4,1024]{2,1,0:T(4,128)S(1)}, ...), condition=%wide.region_7.8_spmd.clone, body=%wide.region_6.7_spmd.clone.sunk | while | flops 16388 | bytes 65645 | solution.py:23
  102.4 0.7 fusion.65
  103.2 0.7 fusion.65
  103.9 0.7 fusion.65
  104.7 1.0 slice_add_fusion
  105.7 3.1 %multiply_reduce_fusion = (f32[8,34]{1,0:T(8,128)S(1)}, f32[8,34,1024]{2,1,0:T(8,128)}) fusion(f32[8,34]{1,0:T(8,128)} %bitcast.33, f32[1024]{0:T(1024)} %copy-done.6, f32[8,34]{1,0:T(8,128)} %bitcast.30, f32[1024]{0:T(1024)} %copy-done.8, f32[8,34,1024]{2,1,0:T(8,128)S(1)} %fusion.9, f32[7,4,1024]{2,1,0:T(4,128)} %slice_add_fusion.5, ...), kind=kOutput, calls=%fused_computation.14 | convolution fusion | flops 15385392 | bytes 2486528 | tf_op jit(solution)/shard_map/kiu,kud->kid/dot_general | solution.py:44
  108.7 2.5 %reshape.92 = f32[272,1024]{1,0:T(8,128)} reshape(f32[8,34,1024]{2,1,0:T(8,128)} %get-tuple-element.149) | data formatting | bytes 2228224 | tf_op jit(solution)/shard_map/reshape | solution.py:110
  111.4 3.1 %fusion.2 = bf16[272,1024]{1,0:T(8,128)(2,1)} fusion(f32[272,1024]{1,0:T(8,128)S(1)} %copy-done.3, bf16[1024,1024]{1,0:T(8,128)(2,1)S(1)} %copy-done, f32[272,1024]{1,0:T(8,128)} %reshape.92, bf16[272,2048]{1,0:T(8,128)(2,1)} %copy-done.5, f32[1024]{0:T(1024)S(1)} %copy-done.23, f32[272]{0:T(512)S(1)} %rsqrt.25), kind=kOutput, calls=%fused_computation.13 | convolution fusion | flops 573489152 | bytes 5444672 | tf_op jit(solution)/shard_map/dot_general | solution.py:114
  114.5 2.1 %all_to_all.32 = bf16[8,34,1024]{2,1,0:T(8,128)(2,1)} reshape(bf16[272,1024]{1,0:T(8,128)(2,1)} %fusion.2) | data formatting | bytes 1114112 | tf_op jit(solution)/shard_map/all_to_all | solution.py:116
  116.6 3.7 %all-to-all-start.3 = ((bf16[8,34,1024]{2,1,0:T(8,128)(2,1)}), bf16[8,34,1024]{2,1,0:T(8,128)(2,1)S(1)}, u32[]{:S(2)}, u32[]{:S(2)}) async-start(bf16[8,34,1024]{2,1,0:T(8,128)(2,1)} %all_to_all.32), calls=%async_computation.3 | async-start | bytes 1310720 | tf_op jit(solution)/shard_map/all_to_all | solution.py:116
  120.2 17.9 %all-to-all-done.3 = bf16[8,34,1024]{2,1,0:T(8,128)(2,1)S(1)} async-done(((bf16[8,34,1024]{2,1,0:T(8,128)(2,1)}), bf16[8,34,1024]{2,1,0:T(8,128)(2,1)S(1)}, u32[]{:S(2)}, u32[]{:S(2)}) %all-to-all-start.3) | async-done | bytes 557088 | tf_op jit(solution)/shard_map/all_to_all | solution.py:116
  138.3 1.6 %gather_fusion = bf16[128,1024]{1,0:T(8,128)(2,1)} fusion(bf16[272,1024]{1,0:T(8,128)(2,1)S(1)} %all_to_all.34, s32[1024]{0:T(1024)S(1)} %pad_clamp_fusion), kind=kCustom, calls=%fused_computation | custom fusion | bytes 524800 | tf_op jit(solution)/shard_map/gather | solution.py:116
  (85 shorter events, 10.1 us)
Async XLA Ops:
  0.0 111.4 %copy-start = (bf16[1024,1024]{1,0:T(8,128)(2,1)S(1)}, bf16[1024,1024]{1,0:T(8,128)(2,1)}, u32[]{:S(2)}) copy-start(bf16[1024,1024]{1,0:T(8,128)(2,1)} %param.19) | copy-start | bytes 6291460
  0.0 14.5 %copy-start.18 = (f32[1024]{0:T(1024)S(1)}, f32[1024]{0:T(1024)}, u32[]{:S(2)}) copy-start(f32[1024]{0:T(1024)} %param.17) | copy-start | bytes 12292
  0.0 14.5 %copy-start.19 = (f32[1024]{0:T(1024)S(1)}, f32[1024]{0:T(1024)}, u32[]{:S(2)}) copy-start(f32[1024]{0:T(1024)} %param.16) | copy-start | bytes 12292
  1.0 26.1 %copy-start.20 = (s32[128]{0:T(128)}, s32[128]{0:T(128)S(1)}, u32[]{:S(2)}) copy-start(s32[128]{0:T(128)S(1)} %compare_select_fusion) | copy-start | bytes 1540
  2.7 13.7 %all-to-all-start.1 = ((s32[8,34,1]{1,2,0:T(1,128)}), s32[8,34,1]{1,2,0:T(1,128)S(1)}, u32[]{:S(2)}, u32[]{:S(2)}) async-start(s32[8,34,1]{1,2,0:T(1,128)} %all_to_all.28), calls=%async_computation.1 | async-start | bytes 8192 | tf_op jit(solution)/shard_map/all_to_all | solution.py:77
  14.5 31.8 %copy-start.6 = (f32[1024]{0:T(1024)}, f32[1024]{0:T(1024)S(1)}, u32[]{:S(2)}) copy-start(f32[1024]{0:T(1024)S(1)} %log.3) | copy-start | bytes 12292
  14.6 31.8 %copy-start.8 = (f32[1024]{0:T(1024)}, f32[1024]{0:T(1024)S(1)}, u32[]{:S(2)}) copy-start(f32[1024]{0:T(1024)S(1)} %neg.11) | copy-start | bytes 12292
  16.4 30.0 %copy-start.10 = (s32[8,34,1]{1,2,0:T(1,128)}, s32[8,34,1]{1,2,0:T(1,128)S(1)}, u32[]{:S(2)}) copy-start(s32[8,34,1]{1,2,0:T(1,128)S(1)} %all-to-all-done.1) | copy-start | bytes 3268
  16.4 10.7 %all-to-all-start.2 = ((s32[8,34,1]{1,2,0:T(1,128)}), s32[8,34,1]{1,2,0:T(1,128)S(1)}, u32[]{:S(2)}, u32[]{:S(2)}) async-start(s32[8,34,1]{1,2,0:T(1,128)} %all_to_all.30), calls=%async_computation.2 | async-start | bytes 8192 | tf_op jit(solution)/shard_map/all_to_all | solution.py:78
  27.1 19.0 %all-to-all-start = ((bf16[8,34,1024]{2,1,0:T(8,128)(2,1)}), bf16[8,34,1024]{2,1,0:T(8,128)(2,1)S(1)}, u32[]{:S(2)}, u32[]{:S(2)}) async-start(bf16[8,34,1024]{2,1,0:T(8,128)(2,1)} %all_to_all.26), calls=%async_computation | async-start | bytes 1310720 | tf_op jit(solution)/shard_map/all_to_all | solution.py:76
  30.8 16.8 %copy-start.14 = (f32[8,4,1]{1,2,0:T(1,128)}, f32[8,4,1]{1,2,0:T(1,128)S(1)}, u32[]{:S(2)}) copy-start(f32[8,4,1]{1,2,0:T(1,128)S(1)} %get-tuple-element.142) | copy-start | bytes 388
  30.9 16.8 %copy-start.16 = (f32[8,4,1]{1,2,0:T(1,128)}, f32[8,4,1]{1,2,0:T(1,128)S(1)}, u32[]{:S(2)}) copy-start(f32[8,4,1]{1,2,0:T(1,128)S(1)} %get-tuple-element.143) | copy-start | bytes 388
  31.8 0.7 copy-start.2
  31.9 15.8 %copy-start.22 = (f32[1024]{0:T(1024)S(1)}, f32[1024]{0:T(1024)}, u32[]{:S(2)}) copy-start(f32[1024]{0:T(1024)} %param.14) | copy-start | bytes 12292
  51.6 1.0 copy-start.5
  53.9 3.0 %copy-start.1 = (f32[8,34,1024]{2,1,0:T(8,128)S(1)}, f32[8,34,1024]{2,1,0:T(8,128)}, u32[]{:S(2)}) copy-start(f32[8,34,1024]{2,1,0:T(8,128)} %reshape.95) | copy-start | bytes 3342340
  53.9 3.0 %copy-start.7 = (f32[1024]{0:T(1024)S(1)}, f32[1024]{0:T(1024)}, u32[]{:S(2)}) copy-start(f32[1024]{0:T(1024)} %copy-done.6) | copy-start | bytes 12292
  53.9 3.0 %copy-start.9 = (f32[1024]{0:T(1024)S(1)}, f32[1024]{0:T(1024)}, u32[]{:S(2)}) copy-start(f32[1024]{0:T(1024)} %copy-done.8) | copy-start | bytes 12292
  53.9 3.0 %copy-start.11 = (s32[8,34,1]{1,2,0:T(1,128)S(1)}, s32[8,34,1]{1,2,0:T(1,128)}, u32[]{:S(2)}) copy-start(s32[8,34,1]{1,2,0:T(1,128)} %copy-done.10) | copy-start | bytes 3268
  53.9 3.0 %copy-start.12 = (f32[8,34,1]{1,2,0:T(1,128)S(1)}, f32[8,34,1]{1,2,0:T(1,128)}, u32[]{:S(2)}) copy-start(f32[8,34,1]{1,2,0:T(1,128)} %get-tuple-element.144) | copy-start | bytes 3268
  53.9 3.0 %copy-start.13 = (f32[8,34,1]{1,2,0:T(1,128)S(1)}, f32[8,34,1]{1,2,0:T(1,128)}, u32[]{:S(2)}) copy-start(f32[8,34,1]{1,2,0:T(1,128)} %get-tuple-element.145) | copy-start | bytes 3268
  53.9 3.0 %copy-start.15 = (f32[8,4,1]{1,2,0:T(1,128)S(1)}, f32[8,4,1]{1,2,0:T(1,128)}, u32[]{:S(2)}) copy-start(f32[8,4,1]{1,2,0:T(1,128)} %copy-done.14) | copy-start | bytes 388
  53.9 3.0 %copy-start.17 = (f32[8,4,1]{1,2,0:T(1,128)S(1)}, f32[8,4,1]{1,2,0:T(1,128)}, u32[]{:S(2)}) copy-start(f32[8,4,1]{1,2,0:T(1,128)} %copy-done.16) | copy-start | bytes 388
  57.8 1.4 copy-start.4
  108.7 2.6 %copy-start.3 = (f32[272,1024]{1,0:T(8,128)S(1)}, f32[272,1024]{1,0:T(8,128)}, u32[]{:S(2)}) copy-start(f32[272,1024]{1,0:T(8,128)} %reshape.93) | copy-start | bytes 3342340
  108.7 2.7 %copy-start.23 = (f32[1024]{0:T(1024)S(1)}, f32[1024]{0:T(1024)}, u32[]{:S(2)}) copy-start(f32[1024]{0:T(1024)} %param.18) | copy-start | bytes 12292
  114.5 5.7 %copy-start.21 = (s32[128]{0:T(128)S(1)}, s32[128]{0:T(128)}, u32[]{:S(2)}) copy-start(s32[128]{0:T(128)} %copy-done.20) | copy-start | bytes 1540
  116.6 21.6 %all-to-all-start.3 = ((bf16[8,34,1024]{2,1,0:T(8,128)(2,1)}), bf16[8,34,1024]{2,1,0:T(8,128)(2,1)S(1)}, u32[]{:S(2)}, u32[]{:S(2)}) async-start(bf16[8,34,1024]{2,1,0:T(8,128)(2,1)} %all_to_all.32), calls=%async_computation.3 | async-start | bytes 1310720 | tf_op jit(solution)/shard_map/all_to_all | solution.py:116
where the time goes:
time: 142 us; the launch traced here: 140 us
  local copies, waits for them, and re-layouts  39.9 us (28%)
  waiting for transfers between devices  37.8 us (27%)
  starting transfers between devices  18.7 us (13%)
  other arithmetic  17.1 us (12%)
  matrix products  14.8 us (10%)
  blocking collectives  10.9 us (8%)
    all_to_all x1, waiting for transfers between devices, on_device(): lax.all_to_all(back_rows, 'shard', split_axis=0, concat_axis=0, tiled=True)  17.9 us
    pad x7, local copies, waits for them, and re-layouts, on_device(): inclusive = lax.associative_scan(combine, (piece_span, piece_ends), axis=0)  15 us
    all_to_all x1, waiting for transfers between devices, on_device(): lax.all_to_all(send_rows, 'shard', split_axis=0, concat_axis=0, tiled=True)  13 us
    all_gather x2, blocking collectives, carried_in(): everything = jax.tree.map(lambda part: lax.all_gather(part, axis), shard)  10.9 us
    dot_general x6, matrix products, exact_einsum(): jnp.einsum(form, left, right.astype(jnp.float32), precision=lax.Precision...  7.64 us
    all_to_all x1, starting transfers between devices, on_device(): lax.all_to_all(send_users, 'shard', split_axis=0, concat_axis=0, tiled=True)  7.28 us
    add x6, other arithmetic, on_device(): inclusive = lax.associative_scan(combine, (piece_span, piece_ends), axis=0)  6.29 us
    all_to_all x1, waiting for transfers between devices, on_device(): lax.all_to_all(send_breaks, 'shard', split_axis=0, concat_axis=0, tiled=T...  5.12 us
  transfers between devices with their start and end apart: 4, of which 4 were waited for; matrix products, arithmetic and copies ran while one was open for 5% of the time, Pallas kernels for 0%

commit v1 on v0

v1 whole, which is shorter than its diff:
```python
import functools

import jax
import jax.numpy as jnp
from jax import lax
from jax.experimental import pallas as pl
from jax.experimental.pallas import tpu as pltpu
from jax.sharding import PartitionSpec as P

U_DEV = 4
LANES = 128
AXES = ("grp", "shard")
F32, BF16 = jnp.float32, jnp.bfloat16


def round_up(value, unit):
    return -(-value // unit) * unit


def dot(left, right):
    return jnp.dot(left, right, preferred_element_type=F32)


def dot_t(left, right):
    return lax.dot_general(left, right, (((0,), (0,)), ((), ())), preferred_element_type=F32)


def rms_rows(values):
    return lax.rsqrt(jnp.mean(values * values, axis=-1, keepdims=True) + 1e-06)


def member_rows(ids_row, users):
    user = lax.broadcasted_iota(jnp.int32, (users, ids_row.shape[1]), 0)
    return (user == ids_row).astype(F32)


def weight_copies(hbm, vmem, sem, chunks, first):
    width = vmem.shape[1] // chunks
    return [
        pltpu.make_async_copy(
            hbm.at[:, pl.ds(first + c * width, width)],
            vmem.at[:, pl.ds(c * width, width)],
            sem.at[c],
        )
        for c in range(chunks)
    ]


def ends_kernel(
    users, rows_used, chunks,
    events, ids, breaks, in_gain, rates, keep, weight,
    payload, normed_out, value_out,
    held, stage, sem,
):
    rows, width = events.shape
    copies = weight_copies(weight, held, sem, chunks, width)
    for copy in copies:
        copy.start()
    ids_row = ids[...]
    break_row = breaks[...].astype(F32)
    member = member_rows(ids_row, users)
    member_b = member.astype(BF16)
    same = dot_t(member_b, member_b)
    after = lax.broadcasted_iota(jnp.int32, (rows, rows), 1) > lax.broadcasted_iota(
        jnp.int32, (rows, rows), 0
    )
    later = jnp.where(after, same, 0.0)
    events_left = jnp.sum(later, axis=1, keepdims=True)
    breaks_left = jnp.sum(later * break_row, axis=1, keepdims=True)
    user_events = jnp.sum(member, axis=1, keepdims=True)
    user_breaks = jnp.sum(member * break_row, axis=1, keepdims=True)
    event_rows = events[...].astype(F32)
    normed = (event_rows * rms_rows(event_rows) * in_gain[...]).astype(BF16)
    normed_out[...] = normed
    splits = width // (rows_used * LANES)
    for s in range(splits):
        stage[:, s, rows_used, :] = jnp.broadcast_to(user_events, (users, LANES))
        stage[:, s, rows_used + 1, :] = jnp.broadcast_to(user_breaks, (users, LANES))
        for r in range(rows_used + 2, stage.shape[2]):
            stage[:, s, r, :] = jnp.zeros((users, LANES), F32)
    block = width // chunks
    for c in range(chunks):
        copies[c].wait()
        cols = pl.ds(c * block, block)
        value = dot(normed, held[:, cols]).astype(BF16)
        value_out[:, cols] = value
        log_left = -rates[:, cols] * events_left + jnp.log(keep[:, cols]) * breaks_left
        faded = (jnp.exp(log_left) * value.astype(F32)).astype(BF16)
        ends = dot(member_b, faded)
        for k in range(block // LANES):
            tile = c * (block // LANES) + k
            stage[:, tile // rows_used, tile % rows_used, :] = ends[:, k * LANES:(k + 1) * LANES]
    payload[...] = stage[...].astype(BF16)


def local_kernel(
    users, chunks,
    normed, value, ids, breaks, rates, keep, out_gain, weight,
    gate_out, growth_out, local_out,
    held, sem,
):
    rows, width = normed.shape
    copies = weight_copies(weight, held, sem, chunks, 0)
    for copy in copies:
        copy.start()
    break_row = breaks[...].astype(F32)
    member_b = member_rows(ids[...], users).astype(BF16)
    same = dot_t(member_b, member_b)
    upto = lax.broadcasted_iota(jnp.int32, (rows, rows), 1) <= lax.broadcasted_iota(
        jnp.int32, (rows, rows), 0
    )
    within = jnp.where(upto, same, 0.0)
    count = jnp.sum(within, axis=1, keepdims=True)
    count_breaks = jnp.sum(within * break_row, axis=1, keepdims=True)
    within_b = within.astype(BF16)
    within_twice = jnp.concatenate([within_b, within_b], axis=1)
    block = width // chunks
    for c in range(chunks):
        cols = pl.ds(c * block, block)
        log_level = -rates[:, cols] * count + jnp.log(keep[:, cols]) * count_breaks
        growth = jnp.exp(log_level)
        growth_out[:, cols] = growth
        scaled = jnp.exp(-log_level) * value[:, cols].astype(F32)
        high = scaled.astype(BF16)
        low = (scaled - high.astype(F32)).astype(BF16)
        local_out[:, cols] = growth * dot(within_twice, jnp.concatenate([high, low], axis=0))
    for c in range(chunks):
        copies[c].wait()
        cols = pl.ds(c * block, block)
        gate = dot(normed[...], held[:, cols]).astype(BF16).astype(F32)
        gate_out[:, cols] = out_gain[:, cols] * (gate / (1.0 + jnp.exp(-gate)))


def prefix_kernel(rows_used, got, rates, keep, carries):
    devices = got.shape[0]
    rate = rates[...]
    log_keep = jnp.log(keep[...])
    pad = carries.shape[1] - rows_used

    def step(d, state):
        block = got[d].astype(F32)
        stored = state
        if pad:
            stored = jnp.concatenate([state, jnp.zeros((pad, LANES), F32)], axis=0)
        carries[d] = stored.astype(BF16)
        span = jnp.exp(
            -rate * block[rows_used:rows_used + 1] + log_keep * block[rows_used + 1:rows_used + 2]
        )
        return span * state + block[:rows_used]

    state = jnp.zeros((rows_used, LANES), F32)
    if devices <= 64:
        for d in range(devices):
            state = step(d, state)
    else:
        lax.fori_loop(0, devices, step, state)


def final_kernel(
    users, rows_used, chunks,
    carries, ids, local, growth, gate, events, weight,
    out,
    held, stage, sem,
):
    rows, width = events.shape
    copies = weight_copies(weight, held, sem, chunks, 0)
    for copy in copies:
        copy.start()
    member_b = member_rows(ids[...], users).astype(BF16)
    stage[...] = carries[...].astype(F32)
    tiles = [
        stage[:, t // rows_used, t % rows_used, :].astype(BF16) for t in range(width // LANES)
    ]
    carry = dot_t(member_b, jnp.concatenate(tiles, axis=1))
    state = local[...] + growth[...] * carry
    mixed_part = (state * rms_rows(state) * gate[...]).astype(BF16)
    block = width // chunks
    for c in range(chunks):
        copies[c].wait()
        cols = pl.ds(c * block, block)
        out[:, cols] = (events[:, cols].astype(F32) + dot(mixed_part, held[:, cols])).astype(BF16)


def on_device(
    devices,
    owners,
    events,
    user_ids,
    session_break,
    in_gain,
    in_weight,
    decay_rates,
    keep_factor,
    out_gain,
    out_weight,
):
    rows, width = events.shape
    users = U_DEV * owners
    rows_used = users * width // (devices * LANES)
    splits = width // (rows_used * LANES)
    rows_out = round_up(rows_used + 2, 8)
    rows_back = round_up(rows_used, 8)
    chunks = 4
    ids = user_ids.reshape(1, rows)
    breaks = session_break.reshape(1, rows)
    row = lambda vector: vector.reshape(1, width)
    hbm = pl.BlockSpec(memory_space=pl.ANY)
    vmem = pl.BlockSpec(memory_space=pltpu.VMEM)
    sds = jax.ShapeDtypeStruct

    payload, normed, value = pl.pallas_call(
        functools.partial(ends_kernel, users, rows_used, chunks),
        out_shape=(
            sds((users, splits, rows_out, LANES), BF16),
            sds((rows, width), BF16),
            sds((rows, width), BF16),
        ),
        in_specs=[vmem] * 6 + [hbm],
        out_specs=(vmem, vmem, vmem),
        scratch_shapes=[
            pltpu.VMEM((width, width), BF16),
            pltpu.VMEM((users, splits, rows_out, LANES), F32),
            pltpu.SemaphoreType.DMA((chunks,)),
        ],
        cost_estimate=pl.CostEstimate(
            flops=2 * rows * width * width, bytes_accessed=2 * width * width, transcendentals=0
        ),
        name="ends",
    )(events, ids, breaks, row(in_gain), row(decay_rates), row(keep_factor), in_weight)
    got = lax.all_to_all(
        payload.reshape(devices, rows_out, LANES), AXES, split_axis=0, concat_axis=0, tiled=True
    )
    gate, growth, local = pl.pallas_call(
        functools.partial(local_kernel, users, chunks),
        out_shape=(sds((rows, width), F32),) * 3,
        in_specs=[vmem] * 7 + [hbm],
        out_specs=(vmem, vmem, vmem),
        scratch_shapes=[
            pltpu.VMEM((width, width), BF16),
            pltpu.SemaphoreType.DMA((chunks,)),
        ],
        cost_estimate=pl.CostEstimate(
            flops=2 * rows * width * width, bytes_accessed=2 * width * width, transcendentals=0
        ),
        name="local",
    )(normed, value, ids, breaks, row(decay_rates), row(keep_factor), row(out_gain), in_weight)
    if splits == 1:
        own = lambda vector: vector.reshape(rows_used, LANES)
    else:
        part = lax.axis_index(AXES) % splits
        own = lambda vector: lax.dynamic_index_in_dim(
            vector.reshape(splits, rows_used, LANES), part, 0, keepdims=False
        )
    carries = pl.pallas_call(
        functools.partial(prefix_kernel, rows_used),
        out_shape=sds((devices, rows_back, LANES), BF16),
        in_specs=[vmem] * 3,
        out_specs=vmem,
        name="prefix",
    )(got, own(decay_rates), own(keep_factor))
    back = lax.all_to_all(carries, AXES, split_axis=0, concat_axis=0, tiled=True)
    return pl.pallas_call(
        functools.partial(final_kernel, users, rows_used, chunks),
        out_shape=sds((rows, width), BF16),
        in_specs=[vmem] * 6 + [hbm],
        out_specs=vmem,
        scratch_shapes=[
            pltpu.VMEM((width, width), BF16),
            pltpu.VMEM((users, splits, rows_back, LANES), F32),
            pltpu.SemaphoreType.DMA((chunks,)),
        ],
        cost_estimate=pl.CostEstimate(
            flops=2 * rows * width * width, bytes_accessed=2 * width * width, transcendentals=0
        ),
        name="final",
    )(back.reshape(users, splits, rows_back, LANES), ids, local, growth, gate, events, out_weight)


def solution(mesh):
    return jax.shard_map(
        functools.partial(on_device, mesh.size, mesh.shape["shard"]),
        mesh=mesh,
        in_specs=(P(AXES, None), P(AXES), P(AXES), P(), P(), P(), P(), P(), P()),
        out_specs=P(AXES, None),
        check_vma=False,
    )
```

time: 142 us -> 36.6 us (0.26); the launches traced: 140 us -> 36.2 us
  local copies, waits for them, and re-layouts: 39.9 us -> 0.62 us
  waiting for transfers between devices: 37.8 us -> 3.02 us
  other arithmetic: 17.1 us -> 0 us
  starting transfers between devices: 18.7 us -> 2.56 us
  matrix products: 14.8 us -> 0 us
  Pallas kernels: 0 us -> 14.7 us
  blocking collectives: 10.9 us -> 15.3 us
    all_to_all x4 -> x1, waiting for transfers between devices: 37.8 us -> 3.02 us  [on_device(): lax.all_to_all(carries, AXES, split_axis=0, concat_axis=0, tiled=True)]
    all_to_all x4 -> x1, starting transfers between devices: 18.7 us -> 2.56 us  [on_device(): lax.all_to_all(carries, AXES, split_axis=0, concat_axis=0, tiled=True)]
    all_to_all x0 -> x1, blocking collectives: none -> 15.3 us  [on_device(): lax.all_to_all(payload.reshape(devices, rows_out, LANES), AXES, split_axi...]
    pad x7 -> x0, local copies, waits for them, and re-layouts: 15 us -> none  [on_device(): inclusive = lax.associative_scan(combine, (piece_span, piece_ends), axis=0)]
    dot_general x9 -> x0, matrix products: 14.8 us -> none  [the longest x6 7.64 us: exact_einsum(): jnp.einsum(form, left, right.astype(jnp.float32), precision=lax.Precision...]
    pallas_call x0 -> x4, Pallas kernels: none -> 14.7 us  [the longest x1 4.45 us: on_device(): pl.pallas_call(functools.partial(ends_kernel, users, rows_used, chunks),...]
    all_gather x2 -> x0, blocking collectives: 10.9 us -> none  [carried_in(): everything = jax.tree.map(lambda part: lax.all_gather(part, axis), shard)]
    add x6 -> x0, other arithmetic: 6.29 us -> none  [on_device(): inclusive = lax.associative_scan(combine, (piece_span, piece_ends), axis=0)]
  transfers between devices with their start and end apart: 4 -> 1, of which waited for: 4 -> 1; matrix products, arithmetic and copies ran while one was open for 5% -> 0% of each run, Pallas kernels for 0% -> 12%
where the time goes in v1:
time: 36.6 us; the launch traced here: 36.2 us
  blocking collectives  15.3 us (42%)
  Pallas kernels  14.7 us (40%)
  waiting for transfers between devices  3.02 us (8%)
  starting transfers between devices  2.56 us (7%)
  local copies, waits for them, and re-layouts  0.62 us (2%)
    all_to_all x1, blocking collectives, on_device(): lax.all_to_all(payload.reshape(devices, rows_out, LANES), AXES, split_axi...  15.3 us
    pallas_call x1, Pallas kernels, on_device(): pl.pallas_call(functools.partial(ends_kernel, users, rows_used, chunks),...  4.45 us
    pallas_call x1, Pallas kernels, on_device(): pl.pallas_call(functools.partial(final_kernel, users, rows_used, chunks),...  4.39 us
    pallas_call x1, Pallas kernels, on_device(): pl.pallas_call(functools.partial(local_kernel, users, chunks), out_shape=...  4.25 us
    all_to_all x1, waiting for transfers between devices, on_device(): lax.all_to_all(carries, AXES, split_axis=0, concat_axis=0, tiled=True)  3.02 us
    all_to_all x1, starting transfers between devices, on_device(): lax.all_to_all(carries, AXES, split_axis=0, concat_axis=0, tiled=True)  2.56 us
    pallas_call x1, Pallas kernels, on_device(): pl.pallas_call(functools.partial(prefix_kernel, rows_used), out_shape=sds...  1.64 us
  transfers between devices with their start and end apart: 1, of which 1 were waited for; matrix products, arithmetic and copies ran while one was open for 0% of the time, Pallas kernels for 12%

profile of v1, /device:TPU:0, one launch (start us, length us, event | category | flops | bytes accessed | tf_op | source)
XLA Modules:
  0.0 36.2 jit_solution(12955982405621288225)
XLA Ops:
  0.0 4.4 %ends.1 = (bf16[32,1,16,128]{3,2,1,0:T(8,128)(2,1)}, bf16[128,1024]{1,0:T(8,128)(2,1)}, bf16[128,1024]{1,0:T(8,128)(2,1)}) custom-call(bf16[128,1024]{1,0:T(8,128)(2,1)} %events.3, s32[1,128]{1,0:T(1,128)} %bitcast.18, s32[1,128]{1,0:T(1,128)} %bitcast.23, f32[1,1024]{1,0:T(1,128)} %bitcast.22, f32[1,1024]{1,0:T(1,128)} %bitcast.12, f32[1,1024]{1,0:T(1,128)} %bitcast.15, ...), custom_call_target="tpu_custom_call" | custom-call | flops 268435456 | bytes 2097152 | tf_op jit(solution)/shard_map/ends/pallas_call | solution.py:211
  4.5 15.3 %all_to_all.10.got = bf16[32,16,128]{2,1,0:T(8,128)(2,1)} all-to-all(bf16[32,16,128]{2,1,0:T(8,128)(2,1)} %bitcast.11), channel_id=1, replica_groups=mesh['grp'=4,'shard'=8] {'grp','shard'}, dimensions={0} | all-to-all | bytes 262144 | tf_op jit(solution)/shard_map/all_to_all | solution.py:230
  19.7 1.6 %prefix.1 = bf16[32,8,128]{2,1,0:T(8,128)(2,1)} custom-call(bf16[32,16,128]{2,1,0:T(8,128)(2,1)} %all_to_all.10.got, f32[8,128]{1,0:T(8,128)} %bitcast.13, f32[8,128]{1,0:T(8,128)} %bitcast.16), custom_call_target="tpu_custom_call" | custom-call | tf_op jit(solution)/shard_map/prefix/pallas_call | solution.py:254
  21.3 2.6 %all-to-all-start.1 = ((bf16[32,8,128]{2,1,0:T(8,128)(2,1)}), bf16[32,8,128]{2,1,0:T(8,128)(2,1)S(1)}, u32[]{:S(2)}, u32[]{:S(2)}) async-start(bf16[32,8,128]{2,1,0:T(8,128)(2,1)} %prefix.1), calls=%async_computation.1 | async-start | bytes 131072 | tf_op jit(solution)/shard_map/all_to_all | solution.py:261
  23.9 4.2 %local.1 = (f32[128,1024]{1,0:T(8,128)}, f32[128,1024]{1,0:T(8,128)}, f32[128,1024]{1,0:T(8,128)}) custom-call(bf16[128,1024]{1,0:T(8,128)(2,1)} %get-tuple-element.12.normed, bf16[128,1024]{1,0:T(8,128)(2,1)} %get-tuple-element.13.value, s32[1,128]{1,0:T(1,128)} %bitcast.19, s32[1,128]{1,0:T(1,128)} %bitcast.24, f32[1,1024]{1,0:T(1,128)} %bitcast.14, ...), custom_call_target="tpu_custom_call" | custom-call | flops 268435456 | bytes 2097152 | tf_op jit(solution)/shard_map/local/pallas_call | solution.py:233
  28.2 3.0 %all-to-all-done.1 = bf16[32,8,128]{2,1,0:T(8,128)(2,1)S(1)} async-done(((bf16[32,8,128]{2,1,0:T(8,128)(2,1)}), bf16[32,8,128]{2,1,0:T(8,128)(2,1)S(1)}, u32[]{:S(2)}, u32[]{:S(2)}) %all-to-all-start.1) | async-done | bytes 65568 | tf_op jit(solution)/shard_map/all_to_all | solution.py:261
  31.2 0.0 copy-start
  31.2 0.6 %copy-done = bf16[32,8,128]{2,1,0:T(8,128)(2,1)} copy-done((bf16[32,8,128]{2,1,0:T(8,128)(2,1)}, bf16[32,8,128]{2,1,0:T(8,128)(2,1)S(1)}, u32[]{:S(2)}) %copy-start) | copy-done | bytes 65560
  31.8 4.4 %final.1 = bf16[128,1024]{1,0:T(8,128)(2,1)} custom-call(bf16[32,1,8,128]{3,2,1,0:T(8,128)(2,1)} %bitcast.10, s32[1,128]{1,0:T(1,128)} %bitcast.20, f32[128,1024]{1,0:T(8,128)} %get-tuple-element.14.local, f32[128,1024]{1,0:T(8,128)} %get-tuple-element.15.growth, f32[128,1024]{1,0:T(8,128)} %get-tuple-element.16.gate, bf16[128,1024]{1,0:T(8,128)(2,1)} %events.3, ...), custom_call_target="tpu_custom_call" | custom-call | flops 268435456 | bytes 2097152 | tf_op jit(solution)/shard_map/final/pallas_call | solution.py:262
Async XLA Ops:
  21.3 9.8 %all-to-all-start.1 = ((bf16[32,8,128]{2,1,0:T(8,128)(2,1)}), bf16[32,8,128]{2,1,0:T(8,128)(2,1)S(1)}, u32[]{:S(2)}, u32[]{:S(2)}) async-start(bf16[32,8,128]{2,1,0:T(8,128)(2,1)} %prefix.1), calls=%async_computation.1 | async-start | bytes 131072 | tf_op jit(solution)/shard_map/all_to_all | solution.py:261
  31.2 0.6 %copy-start = (bf16[32,8,128]{2,1,0:T(8,128)(2,1)}, bf16[32,8,128]{2,1,0:T(8,128)(2,1)S(1)}, u32[]{:S(2)}) copy-start(bf16[32,8,128]{2,1,0:T(8,128)(2,1)S(1)} %all-to-all-done.1) | copy-start | bytes 196612

commit v2 on v1

v2 whole, which is shorter than its diff:
```python
import functools

import jax
import jax.numpy as jnp
from jax import lax
from jax.experimental import pallas as pl
from jax.experimental.pallas import tpu as pltpu
from jax.sharding import PartitionSpec as P

U_DEV = 4
LANES = 128
CHUNKS = 4
VMEM_BYTES = 12 * 2**20
AXES = ("grp", "shard")
F32, BF16 = jnp.float32, jnp.bfloat16


def round_up(value, unit):
    return -(-value // unit) * unit


def dot(left, right):
    return jnp.dot(left, right, preferred_element_type=F32)


def dot_t(left, right):
    return lax.dot_general(left, right, (((0,), (0,)), ((), ())), preferred_element_type=F32)


def rms_rows(values):
    return lax.rsqrt(jnp.mean(values * values, axis=-1, keepdims=True) + 1e-06)


def normed_rows(events, in_gain):
    event_rows = events[...].astype(F32)
    return (event_rows * rms_rows(event_rows) * in_gain[...]).astype(BF16)


def member_rows(ids_row, users):
    user = lax.broadcasted_iota(jnp.int32, (users, ids_row.shape[1]), 0)
    return (user == ids_row).astype(F32)


def started(copies):
    for copy in copies:
        copy.start()
    return copies


def weight_copies(hbm, vmem, sem, chunks, first):
    width = vmem.shape[1] // chunks
    return [
        pltpu.make_async_copy(
            hbm.at[:, pl.ds(first + c * width, width)],
            vmem.at[:, pl.ds(c * width, width)],
            sem.at[c],
        )
        for c in range(chunks)
    ]


def ends_kernel(
    users, rows_used,
    events_hbm, ids_hbm, breaks_hbm, in_gain_hbm, rates_hbm, keep_hbm, weight_hbm,
    payload,
    events, ids, breaks, in_gain, rates, keep, held, stage, small_sem, sem,
):
    rows, width = events.shape
    small = started(
        [
            pltpu.make_async_copy(source, target, small_sem.at[i])
            for i, (source, target) in enumerate(
                (
                    (events_hbm, events),
                    (ids_hbm, ids),
                    (breaks_hbm, breaks),
                    (in_gain_hbm, in_gain),
                    (rates_hbm, rates),
                    (keep_hbm, keep),
                )
            )
        ]
    )
    copies = started(weight_copies(weight_hbm, held, sem, CHUNKS, width))
    for copy in small:
        copy.wait()
    break_row = breaks[...].astype(F32)
    member = member_rows(ids[...], users)
    member_b = member.astype(BF16)
    same = dot_t(member_b, member_b)
    after = lax.broadcasted_iota(jnp.int32, (rows, rows), 1) > lax.broadcasted_iota(
        jnp.int32, (rows, rows), 0
    )
    later = jnp.where(after, same, 0.0)
    events_left = jnp.sum(later, axis=1, keepdims=True)
    breaks_left = jnp.sum(later * break_row, axis=1, keepdims=True)
    user_events = jnp.sum(member, axis=1, keepdims=True)
    user_breaks = jnp.sum(member * break_row, axis=1, keepdims=True)
    normed = normed_rows(events, in_gain)
    splits = width // (rows_used * LANES)
    for s in range(splits):
        stage[:, s, rows_used, :] = jnp.broadcast_to(user_events, (users, LANES))
        stage[:, s, rows_used + 1, :] = jnp.broadcast_to(user_breaks, (users, LANES))
        for r in range(rows_used + 2, stage.shape[2]):
            stage[:, s, r, :] = jnp.zeros((users, LANES), F32)
    block = width // CHUNKS
    for c in range(CHUNKS):
        cols = pl.ds(c * block, block)
        fade = jnp.exp(-rates[:, cols] * events_left + jnp.log(keep[:, cols]) * breaks_left)
        copies[c].wait()
        value = dot(normed, held[:, cols]).astype(BF16)
        ends = dot(member_b, (fade * value.astype(F32)).astype(BF16))
        for k in range(block // LANES):
            tile = c * (block // LANES) + k
            stage[:, tile // rows_used, tile % rows_used, :] = ends[:, k * LANES:(k + 1) * LANES]
    payload[...] = stage[...].astype(BF16)


def local_kernel(
    users,
    events, ids, breaks, in_gain, rates, keep, out_gain, weight_hbm,
    held_back,
    held, sem,
):
    rows, width = events.shape
    copies = started(weight_copies(weight_hbm, held, sem, 2 * CHUNKS, 0))
    break_row = breaks[...].astype(F32)
    member_b = member_rows(ids[...], users).astype(BF16)
    same = dot_t(member_b, member_b)
    upto = lax.broadcasted_iota(jnp.int32, (rows, rows), 1) <= lax.broadcasted_iota(
        jnp.int32, (rows, rows), 0
    )
    within = jnp.where(upto, same, 0.0)
    count = jnp.sum(within, axis=1, keepdims=True)
    count_breaks = jnp.sum(within * break_row, axis=1, keepdims=True)
    within_b = within.astype(BF16)
    within_twice = jnp.concatenate([within_b, within_b], axis=1)
    normed = normed_rows(events, in_gain)
    block = width // CHUNKS
    for c in range(CHUNKS):
        copies[c].wait()
        cols = pl.ds(c * block, block)
        gate = dot(normed, held[:, cols]).astype(BF16).astype(F32)
        held_back[0, :, cols] = out_gain[:, cols] * (gate / (1.0 + jnp.exp(-gate)))
    for c in range(CHUNKS):
        cols = pl.ds(c * block, block)
        log_level = -rates[:, cols] * count + jnp.log(keep[:, cols]) * count_breaks
        growth = jnp.exp(log_level)
        held_back[1, :, cols] = growth
        copies[CHUNKS + c].wait()
        value = dot(normed, held[:, pl.ds(width + c * block, block)]).astype(BF16)
        scaled = jnp.exp(-log_level) * value.astype(F32)
        high = scaled.astype(BF16)
        low = (scaled - high.astype(F32)).astype(BF16)
        held_back[2, :, cols] = growth * dot(within_twice, jnp.concatenate([high, low], axis=0))


def prefix_kernel(rows_used, got, rates, keep, carries):
    devices = got.shape[0]
    rate = rates[...]
    log_keep = jnp.log(keep[...])
    pad = carries.shape[1] - rows_used

    def step(d, state):
        block = got[d].astype(F32)
        stored = state
        if pad:
            stored = jnp.concatenate([state, jnp.zeros((pad, LANES), F32)], axis=0)
        carries[d] = stored.astype(BF16)
        span = jnp.exp(
            -rate * block[rows_used:rows_used + 1] + log_keep * block[rows_used + 1:rows_used + 2]
        )
        return span * state + block[:rows_used]

    state = jnp.zeros((rows_used, LANES), F32)
    if devices <= 64:
        for d in range(devices):
            state = step(d, state)
    else:
        lax.fori_loop(0, devices, step, state)


def final_kernel(
    users, rows_used,
    carries, ids, held_back, events_hbm, weight_hbm,
    out,
    events, held, stage, small_sem, sem,
):
    rows, width = events.shape
    copies = started(weight_copies(weight_hbm, held, sem, CHUNKS, 0))
    (events_copy,) = started([pltpu.make_async_copy(events_hbm, events, small_sem)])
    member_b = member_rows(ids[...], users).astype(BF16)
    stage[...] = carries[...].astype(F32)
    tiles = [
        stage[:, t // rows_used, t % rows_used, :].astype(BF16) for t in range(width // LANES)
    ]
    carry = dot_t(member_b, jnp.concatenate(tiles, axis=1))
    state = held_back[2] + held_back[1] * carry
    mixed_part = (state * rms_rows(state) * held_back[0]).astype(BF16)
    block = width // CHUNKS
    events_copy.wait()
    for c in range(CHUNKS):
        copies[c].wait()
        cols = pl.ds(c * block, block)
        out[:, cols] = (events[:, cols].astype(F32) + dot(mixed_part, held[:, cols])).astype(BF16)


def on_device(
    devices,
    owners,
    events,
    user_ids,
    session_break,
    in_gain,
    in_weight,
    decay_rates,
    keep_factor,
    out_gain,
    out_weight,
):
    rows, width = events.shape
    users = U_DEV * owners
    rows_used = users * width // (devices * LANES)
    splits = width // (rows_used * LANES)
    rows_out = round_up(rows_used + 2, 8)
    rows_back = round_up(rows_used, 8)
    ids = user_ids.reshape(1, rows)
    breaks = session_break.reshape(1, rows)
    row = lambda vector: vector.reshape(1, width)
    hbm = pl.BlockSpec(memory_space=pltpu.HBM)
    vmem = pl.BlockSpec(memory_space=pltpu.VMEM)
    in_hbm = lambda value: pltpu.with_memory_space_constraint(value, pltpu.HBM)
    sds = jax.ShapeDtypeStruct
    params = pltpu.CompilerParams(vmem_limit_bytes=VMEM_BYTES)
    half = pl.CostEstimate(
        flops=2 * rows * width * width, bytes_accessed=2 * width * width, transcendentals=0
    )
    whole = pl.CostEstimate(
        flops=4 * rows * width * width, bytes_accessed=4 * width * width, transcendentals=0
    )

    payload = pl.pallas_call(
        functools.partial(ends_kernel, users, rows_used),
        out_shape=sds((users, splits, rows_out, LANES), BF16),
        in_specs=[hbm] * 7,
        out_specs=vmem,
        scratch_shapes=[
            pltpu.VMEM((rows, width), BF16),
            pltpu.VMEM((1, rows), jnp.int32),
            pltpu.VMEM((1, rows), jnp.int32),
            pltpu.VMEM((1, width), F32),
            pltpu.VMEM((1, width), F32),
            pltpu.VMEM((1, width), F32),
            pltpu.VMEM((width, width), BF16),
            pltpu.VMEM((users, splits, rows_out, LANES), F32),
            pltpu.SemaphoreType.DMA((6,)),
            pltpu.SemaphoreType.DMA((CHUNKS,)),
        ],
        cost_estimate=half,
        compiler_params=params,
        name="ends",
    )(*map(in_hbm, (events, ids, breaks, row(in_gain), row(decay_rates), row(keep_factor), in_weight)))
    got = lax.all_to_all(
        payload.reshape(devices, rows_out, LANES), AXES, split_axis=0, concat_axis=0, tiled=True
    )
    held_back = pl.pallas_call(
        functools.partial(local_kernel, users),
        out_shape=sds((3, rows, width), F32),
        in_specs=[vmem] * 7 + [hbm],
        out_specs=vmem,
        scratch_shapes=[
            pltpu.VMEM((width, 2 * width), BF16),
            pltpu.SemaphoreType.DMA((2 * CHUNKS,)),
        ],
        cost_estimate=whole,
        compiler_params=params,
        name="local",
    )(
        events, ids, breaks, row(in_gain), row(decay_rates), row(keep_factor), row(out_gain),
        in_hbm(in_weight),
    )
    if splits == 1:
        own = lambda vector: vector.reshape(rows_used, LANES)
    else:
        part = lax.axis_index(AXES) % splits
        own = lambda vector: lax.dynamic_index_in_dim(
            vector.reshape(splits, rows_used, LANES), part, 0, keepdims=False
        )
    carries = pl.pallas_call(
        functools.partial(prefix_kernel, rows_used),
        out_shape=sds((devices, rows_back, LANES), BF16),
        in_specs=[vmem] * 3,
        out_specs=vmem,
        compiler_params=params,
        name="prefix",
    )(got, own(decay_rates), own(keep_factor))
    back = lax.all_to_all(carries, AXES, split_axis=0, concat_axis=0, tiled=True)
    return pl.pallas_call(
        functools.partial(final_kernel, users, rows_used),
        out_shape=sds((rows, width), BF16),
        in_specs=[vmem] * 3 + [hbm] * 2,
        out_specs=vmem,
        scratch_shapes=[
            pltpu.VMEM((rows, width), BF16),
            pltpu.VMEM((width, width), BF16),
            pltpu.VMEM((users, splits, rows_back, LANES), F32),
            pltpu.SemaphoreType.DMA(()),
            pltpu.SemaphoreType.DMA((CHUNKS,)),
        ],
        cost_estimate=half,
        compiler_params=params,
        name="final",
    )(back.reshape(users, splits, rows_back, LANES), ids, held_back, in_hbm(events),
      in_hbm(out_weight))


def solution(mesh):
    return jax.shard_map(
        functools.partial(on_device, mesh.size, mesh.shape["shard"]),
        mesh=mesh,
        in_specs=(P(AXES, None), P(AXES), P(AXES), P(), P(), P(), P(), P(), P()),
        out_specs=P(AXES, None),
        check_vma=False,
    )
```

time: 36.6 us -> 32.3 us (0.88)
  Pallas kernels: 14.7 us -> 11.6 us
  local copies, waits for them, and re-layouts: 0.62 us -> 0.03 us
    pallas_call x3, Pallas kernels: 13.1 us -> 10.9 us  [the longest x1 4.31 us: on_device(): pl.pallas_call(functools.partial(local_kernel, users), out_shape=sds((3,...]
    pallas_call x1, Pallas kernels: 1.64 us -> 0.71 us  [on_device(): pl.pallas_call(functools.partial(prefix_kernel, rows_used), out_shape=sds...]
    unnamed x2 -> x14, local copies, waits for them, and re-layouts: 0.62 us -> 0.03 us
  transfers between devices with their start and end apart: 1 -> 1, of which waited for: 1 -> 1; matrix products, arithmetic and copies ran while one was open for 0% -> 0% of each run, Pallas kernels for 12% -> 13%
where the time goes in v2:
time: 32.3 us; the launch traced here: 32.1 us
  blocking collectives  15 us (46%)
  Pallas kernels  11.6 us (36%)
  waiting for transfers between devices  2.91 us (9%)
  starting transfers between devices  2.57 us (8%)
    all_to_all x1, blocking collectives, on_device(): lax.all_to_all(payload.reshape(devices, rows_out, LANES), AXES, split_axi...  15 us
    pallas_call x1, Pallas kernels, on_device(): pl.pallas_call(functools.partial(local_kernel, users), out_shape=sds((3,...  4.31 us
    pallas_call x1, Pallas kernels, on_device(): pl.pallas_call(functools.partial(ends_kernel, users, rows_used), out_shap...  3.51 us
    pallas_call x1, Pallas kernels, on_device(): pl.pallas_call(functools.partial(final_kernel, users, rows_used), out_sha...  3.04 us
    all_to_all x1, waiting for transfers between devices, on_device(): lax.all_to_all(carries, AXES, split_axis=0, concat_axis=0, tiled=True)  2.91 us
    all_to_all x1, starting transfers between devices, on_device(): lax.all_to_all(carries, AXES, split_axis=0, concat_axis=0, tiled=True)  2.57 us
    pallas_call x1, Pallas kernels, on_device(): pl.pallas_call(functools.partial(prefix_kernel, rows_used), out_shape=sds...  0.71 us
  transfers between devices with their start and end apart: 1, of which 1 were waited for; matrix products, arithmetic and copies ran while one was open for 0% of the time, Pallas kernels for 13%

profile of v2, /device:TPU:0, one launch (start us, length us, event | category | flops | bytes accessed | tf_op | source)
XLA Modules:
  0.0 32.1 jit_solution(10789218547151040271)
XLA Ops:
  0.0 0.0 copy-start.1
  0.0 0.0 copy-start.2
  0.0 0.0 copy-start
  0.0 0.0 copy-start.3
  0.0 0.0 copy-start.4
  0.0 0.0 copy-start.5
  0.0 0.0 copy-start.6
  0.0 3.5 %ends.1 = bf16[32,1,16,128]{3,2,1,0:T(8,128)(2,1)S(1)} custom-call(bf16[128,1024]{1,0:T(8,128)(2,1)} %events_hbm.3, s32[1,128]{1,0:T(1,128)} %bitcast.20, s32[1,128]{1,0:T(1,128)} %bitcast.24, f32[1,1024]{1,0:T(1,128)} %bitcast.18, f32[1,1024]{1,0:T(1,128)} %bitcast.12, f32[1,1024]{1,0:T(1,128)} %bitcast.15, bf16[1024,2048]{1,0:T(8,128)(2,1)} %weight_hbm.4), custom_call_target="tpu_custom_call" | custom-call | flops 268435456 | bytes 2097152 | tf_op jit(solution)/shard_map/ends/pallas_call | solution.py:242
  3.6 15.0 %all_to_all.10.got = bf16[32,16,128]{2,1,0:T(8,128)(2,1)S(1)} all-to-all(bf16[32,16,128]{2,1,0:T(8,128)(2,1)S(1)} %bitcast.10), channel_id=1, replica_groups=mesh['grp'=4,'shard'=8] {'grp','shard'}, dimensions={0} | all-to-all | bytes 262144 | tf_op jit(solution)/shard_map/all_to_all | solution.py:263
  18.5 0.0 copy-done.1
  18.5 0.0 copy-done.2
  18.5 0.7 %prefix.1 = bf16[32,8,128]{2,1,0:T(8,128)(2,1)} custom-call(bf16[32,16,128]{2,1,0:T(8,128)(2,1)S(1)} %all_to_all.10.got, f32[8,128]{1,0:T(8,128)S(1)} %bitcast.13, f32[8,128]{1,0:T(8,128)S(1)} %bitcast.16), custom_call_target="tpu_custom_call" | custom-call | tf_op jit(solution)/shard_map/prefix/pallas_call | solution.py:289
  19.2 2.6 %all-to-all-start.1 = ((bf16[32,8,128]{2,1,0:T(8,128)(2,1)}), bf16[32,8,128]{2,1,0:T(8,128)(2,1)S(1)}, u32[]{:S(2)}, u32[]{:S(2)}) async-start(bf16[32,8,128]{2,1,0:T(8,128)(2,1)} %prefix.1), calls=%async_computation.1 | async-start | bytes 131072 | tf_op jit(solution)/shard_map/all_to_all | solution.py:297
  21.8 0.0 copy-done
  21.8 0.0 copy-done.3
  21.8 0.0 copy-done.4
  21.8 0.0 copy-done.5
  21.9 0.0 copy-done.6
  21.9 4.3 %local.1.held_back = f32[3,128,1024]{2,1,0:T(8,128)S(1)} custom-call(bf16[128,1024]{1,0:T(8,128)(2,1)S(1)} %copy-done, s32[1,128]{1,0:T(1,128)S(1)} %bitcast.21, s32[1,128]{1,0:T(1,128)S(1)} %bitcast.25, f32[1,1024]{1,0:T(1,128)S(1)} %bitcast.19, f32[1,1024]{1,0:T(1,128)S(1)} %bitcast.14, f32[1,1024]{1,0:T(1,128)S(1)} %bitcast.17, f32[1,1024]{1,0:T(1,128)S(1)} %bitcast.23, ...), custom_call_target="tpu_custom_call" | custom-call | flops 536870912 | bytes 4194304 | tf_op jit(solution)/shard_map/local/pallas_call | solution.py:266
  26.2 2.9 %all-to-all-done.1 = bf16[32,8,128]{2,1,0:T(8,128)(2,1)S(1)} async-done(((bf16[32,8,128]{2,1,0:T(8,128)(2,1)}), bf16[32,8,128]{2,1,0:T(8,128)(2,1)S(1)}, u32[]{:S(2)}, u32[]{:S(2)}) %all-to-all-start.1) | async-done | bytes 65568 | tf_op jit(solution)/shard_map/all_to_all | solution.py:297
  29.1 3.0 %final.1 = bf16[128,1024]{1,0:T(8,128)(2,1)} custom-call(bf16[32,1,8,128]{3,2,1,0:T(8,128)(2,1)S(1)} %bitcast.11, s32[1,128]{1,0:T(1,128)S(1)} %bitcast.22, f32[3,128,1024]{2,1,0:T(8,128)S(1)} %local.1.held_back, bf16[128,1024]{1,0:T(8,128)(2,1)} %events_hbm.3, bf16[1024,1024]{1,0:T(8,128)(2,1)} %weight_hbm.5), custom_call_target="tpu_custom_call" | custom-call | flops 268435456 | bytes 2097152 | tf_op jit(solution)/shard_map/final/pallas_call | solution.py:298
Async XLA Ops:
  0.0 18.5 %copy-start.1 = (f32[1024]{0:T(1024)S(1)}, f32[1024]{0:T(1024)}, u32[]{:S(2)}) copy-start(f32[1024]{0:T(1024)} %param.14) | copy-start | bytes 12292
  0.0 18.5 %copy-start.2 = (f32[1024]{0:T(1024)S(1)}, f32[1024]{0:T(1024)}, u32[]{:S(2)}) copy-start(f32[1024]{0:T(1024)} %param.15) | copy-start | bytes 12292
  0.0 21.8 %copy-start = (bf16[128,1024]{1,0:T(8,128)(2,1)S(1)}, bf16[128,1024]{1,0:T(8,128)(2,1)}, u32[]{:S(2)}) copy-start(bf16[128,1024]{1,0:T(8,128)(2,1)} %events_hbm.3) | copy-start | bytes 786436
  0.0 21.8 %copy-start.3 = (f32[1024]{0:T(1024)S(1)}, f32[1024]{0:T(1024)}, u32[]{:S(2)}) copy-start(f32[1024]{0:T(1024)} %param.12) | copy-start | bytes 12292
  0.0 21.8 %copy-start.4 = (s32[128]{0:T(128)S(1)}, s32[128]{0:T(128)}, u32[]{:S(2)}) copy-start(s32[128]{0:T(128)} %param.10) | copy-start | bytes 1540
  0.0 21.8 %copy-start.5 = (f32[1024]{0:T(1024)S(1)}, f32[1024]{0:T(1024)}, u32[]{:S(2)}) copy-start(f32[1024]{0:T(1024)} %param.16) | copy-start | bytes 12292
  0.0 21.8 %copy-start.6 = (s32[128]{0:T(128)S(1)}, s32[128]{0:T(128)}, u32[]{:S(2)}) copy-start(s32[128]{0:T(128)} %param.11) | copy-start | bytes 1540
  19.2 9.9 %all-to-all-start.1 = ((bf16[32,8,128]{2,1,0:T(8,128)(2,1)}), bf16[32,8,128]{2,1,0:T(8,128)(2,1)S(1)}, u32[]{:S(2)}, u32[]{:S(2)}) async-start(bf16[32,8,128]{2,1,0:T(8,128)(2,1)} %prefix.1), calls=%async_computation.1 | async-start | bytes 131072 | tf_op jit(solution)/shard_map/all_to_all | solution.py:297

commit v3 on v2

v3 whole, which is shorter than its diff:
```python
import functools

import jax
import jax.numpy as jnp
from jax import lax
from jax.experimental import pallas as pl
from jax.experimental.pallas import tpu as pltpu
from jax.sharding import PartitionSpec as P

U_DEV = 4
LANES = 128
CHUNKS = 4
RADIX = 128.0
VMEM_BYTES = 12 * 2**20
AXES = ("grp", "shard")
F32, BF16 = jnp.float32, jnp.bfloat16


def dot(left, right):
    return jnp.dot(left, right, preferred_element_type=F32)


def dot_t(left, right):
    return lax.dot_general(left, right, (((0,), (0,)), ((), ())), preferred_element_type=F32)


def rms_rows(values):
    return lax.rsqrt(jnp.mean(values * values, axis=-1, keepdims=True) + 1e-06)


def member_rows(ids_row, users):
    user = lax.broadcasted_iota(jnp.int32, (users, ids_row.shape[1]), 0)
    return (user == ids_row).astype(F32)


def row_compare(rows, compare):
    square = (rows, rows)
    return compare(
        lax.broadcasted_iota(jnp.int32, square, 1), lax.broadcasted_iota(jnp.int32, square, 0)
    )


def as_lanes(columns):
    shape = (columns[0].shape[0], LANES)
    lane = lax.broadcasted_iota(jnp.int32, shape, 1)
    total = jnp.zeros(shape, F32)
    for i, column in enumerate(columns):
        total = jnp.where(lane == i, column, total)
    return total


def started(copies):
    for copy in copies:
        copy.start()
    return copies


def weight_copies(hbm, vmem, sem, first):
    chunks = sem.shape[0]
    width = vmem.shape[1] // chunks
    return [
        pltpu.make_async_copy(
            hbm.at[:, pl.ds(first + c * width, width)],
            vmem.at[:, pl.ds(c * width, width)],
            sem.at[c],
        )
        for c in range(chunks)
    ]


def write_message(message, totals, events, breaks):
    width = totals.shape[1]
    message[:, :width] = totals.astype(BF16)
    high_events = jnp.floor(events * (1.0 / RADIX))
    high_breaks = jnp.floor(breaks * (1.0 / RADIX))
    message[:, width:] = as_lanes(
        [high_events, events - RADIX * high_events, high_breaks, breaks - RADIX * high_breaks]
    ).astype(BF16)


def ends_kernel(
    users,
    events_hbm, ids_hbm, breaks_hbm, in_gain_hbm, rates_hbm, keep_hbm, weight_hbm,
    message, totals, counts, normed_out, value_out,
    events, ids, breaks, in_gain, rates, keep, held, small_sem, sem,
):
    rows, width = events.shape
    small = started(
        [
            pltpu.make_async_copy(source, target, small_sem.at[i])
            for i, (source, target) in enumerate(
                (
                    (events_hbm, events),
                    (ids_hbm, ids),
                    (breaks_hbm, breaks),
                    (in_gain_hbm, in_gain),
                    (rates_hbm, rates),
                    (keep_hbm, keep),
                )
            )
        ]
    )
    copies = started(weight_copies(weight_hbm, held, sem, width))
    for copy in small:
        copy.wait()
    break_row = breaks[...].astype(F32)
    member = member_rows(ids[...], users)
    member_b = member.astype(BF16)
    later = jnp.where(row_compare(rows, jnp.greater), dot_t(member_b, member_b), 0.0)
    events_left = jnp.sum(later, axis=1, keepdims=True)
    breaks_left = jnp.sum(later * break_row, axis=1, keepdims=True)
    user_events = jnp.sum(member, axis=1, keepdims=True)
    user_breaks = jnp.sum(member * break_row, axis=1, keepdims=True)
    counts[...] = as_lanes([user_events, user_breaks])
    event_rows = events[...].astype(F32)
    normed = (event_rows * rms_rows(event_rows) * in_gain[...]).astype(BF16)
    normed_out[...] = normed
    block = width // CHUNKS
    for c in range(CHUNKS):
        cols = pl.ds(c * block, block)
        fade = jnp.exp(-rates[:, cols] * events_left + jnp.log(keep[:, cols]) * breaks_left)
        copies[c].wait()
        value = dot(normed, held[:, cols]).astype(BF16)
        value_out[:, cols] = value
        totals[:, cols] = dot(member_b, (fade * value.astype(F32)).astype(BF16))
    write_message(message, totals[...], user_events, user_breaks)


def gate_kernel(normed, out_gain, weight_hbm, gate_out, held, sem):
    width = normed.shape[1]
    copies = started(weight_copies(weight_hbm, held, sem, 0))
    block = width // CHUNKS
    for c in range(CHUNKS):
        copies[c].wait()
        cols = pl.ds(c * block, block)
        gate = dot(normed[...], held[:, cols]).astype(BF16).astype(F32)
        gate_out[:, cols] = out_gain[:, cols] * (gate / (1.0 + jnp.exp(-gate)))


def local_kernel(users, value, ids, breaks, rates, keep, level_out, local_out):
    rows, width = value.shape
    break_row = breaks[...].astype(F32)
    member_b = member_rows(ids[...], users).astype(BF16)
    within = jnp.where(row_compare(rows, jnp.less_equal), dot_t(member_b, member_b), 0.0)
    count = jnp.sum(within, axis=1, keepdims=True)
    count_breaks = jnp.sum(within * break_row, axis=1, keepdims=True)
    level_out[...] = as_lanes([count, count_breaks])
    within_b = within.astype(BF16)
    within_twice = jnp.concatenate([within_b, within_b], axis=1)
    scaled = jnp.exp(rates[...] * count - jnp.log(keep[...]) * count_breaks) * value[...].astype(F32)
    high = scaled.astype(BF16)
    low = (scaled - high.astype(F32)).astype(BF16)
    local_out[...] = dot(within_twice, jnp.concatenate([high, low], axis=0))


def merged(axis, stride, size, messages, totals, counts, carry, rates, keep, need_totals):
    width = totals.shape[1]
    place = lax.rem(lax.div(lax.axis_index(axis), stride), size)
    rate, log_keep = rates[...], jnp.log(keep[...])
    level = lambda events, breaks: log_keep * breaks - rate * events
    column = lambda array, i: array[:, i:i + 1]
    events, breaks, carry_events, carry_breaks = (column(counts, i) for i in range(4))

    def fold(step, state):
        totals, events, breaks, carry, carry_events, carry_breaks = state
        got = messages[step - 1][...].astype(F32)
        got_totals, digits = got[:, :width], got[:, width:]
        got_events = RADIX * column(digits, 0) + column(digits, 1)
        got_breaks = RADIX * column(digits, 2) + column(digits, 3)
        earlier = (place >= step).astype(F32)
        fade = earlier * jnp.exp(level(carry_events, carry_breaks))
        carry = fade * got_totals if carry is None else carry + fade * got_totals
        if need_totals:
            after = 1.0 - earlier
            totals = (
                jnp.exp(level(earlier * events, earlier * breaks)) * got_totals
                + jnp.exp(level(after * got_events, after * got_breaks)) * totals
            )
        return (
            totals, events + got_events, breaks + got_breaks,
            carry, carry_events + earlier * got_events, carry_breaks + earlier * got_breaks,
        )

    state = (totals, events, breaks, carry, carry_events, carry_breaks)
    for step in range(1, size):
        state = fold(step, state)
    return state


def merge_kernel(axis, stride, size, fresh, *refs):
    messages, (totals, counts, *rest) = refs[:size - 1], refs[size - 1:]
    carry = None if fresh else rest.pop(0)[...]
    rates, keep, message, totals_out, counts_out, carry_out = rest
    state = merged(
        axis, stride, size, messages, totals[...], counts[...], carry, rates, keep, True
    )
    new_totals, events, breaks, new_carry, carry_events, carry_breaks = state
    write_message(message, new_totals, events, breaks)
    totals_out[...] = new_totals
    counts_out[...] = as_lanes([events, breaks, carry_events, carry_breaks])
    carry_out[...] = new_carry


def final_kernel(axis, stride, size, users, *refs):
    messages, rest = refs[:size - 1], refs[size - 1:]
    totals, counts, carry, rates, keep, ids, level, local, gate, events, weight, out = rest
    width = events.shape[1]
    state = merged(
        axis, stride, size, messages, totals[...], counts[...], carry[...], rates, keep, False
    )
    carried = state[3]
    high = carried.astype(BF16)
    low = (carried - high.astype(F32)).astype(BF16)
    member_b = member_rows(ids[...], users).astype(BF16)
    entering = dot_t(
        jnp.concatenate([member_b, member_b], axis=0), jnp.concatenate([high, low], axis=0)
    )
    growth = jnp.exp(jnp.log(keep[...]) * level[:, 1:2] - rates[...] * level[:, 0:1])
    hidden = growth * (local[...] + entering)
    mixed_part = (hidden * rms_rows(hidden) * gate[...]).astype(BF16)
    block = width // CHUNKS
    for c in range(CHUNKS):
        cols = pl.ds(c * block, block)
        out[:, cols] = (events[:, cols].astype(F32) + dot(mixed_part, weight[:, cols])).astype(BF16)


def exchange_rounds(mesh):
    rounds = []
    for axis in reversed(AXES):
        stride, left, size = 1, mesh.shape[axis], 2
        while left > 1:
            if left % size:
                size += 1
                continue
            rounds.append((axis, stride, size))
            stride, left = stride * size, left // size
    return rounds


def shift_pairs(length, stride, size, step):
    pairs = []
    for source in range(length):
        place = source // stride % size
        pairs.append((source, source + ((place + step) % size - place) * stride))
    return pairs


def on_device(
    mesh_shape,
    rounds,
    events,
    user_ids,
    session_break,
    in_gain,
    in_weight,
    decay_rates,
    keep_factor,
    out_gain,
    out_weight,
):
    rows, width = events.shape
    users = U_DEV * mesh_shape["shard"]
    ids = user_ids.reshape(1, rows)
    breaks = session_break.reshape(1, rows)
    row = lambda vector: vector.reshape(1, width)
    gain, rates, keep = row(in_gain), row(decay_rates), row(keep_factor)
    hbm = pl.BlockSpec(memory_space=pltpu.HBM)
    vmem = pl.BlockSpec(memory_space=pltpu.VMEM)
    in_hbm = lambda value: pltpu.with_memory_space_constraint(value, pltpu.HBM)
    sds = jax.ShapeDtypeStruct
    params = pltpu.CompilerParams(vmem_limit_bytes=VMEM_BYTES)
    matmul_cost = pl.CostEstimate(
        flops=2 * rows * width * width, bytes_accessed=2 * width * width, transcendentals=0
    )
    message_type = sds((users, width + LANES), BF16)
    state_type = sds((users, width), F32)
    counts_type = sds((users, LANES), F32)

    message, totals, counts, normed, value = pl.pallas_call(
        functools.partial(ends_kernel, users),
        out_shape=(
            message_type, state_type, counts_type, sds((rows, width), BF16), sds((rows, width), BF16)
        ),
        in_specs=[hbm] * 7,
        out_specs=(vmem,) * 5,
        scratch_shapes=[
            pltpu.VMEM((rows, width), BF16),
            pltpu.VMEM((1, rows), jnp.int32),
            pltpu.VMEM((1, rows), jnp.int32),
            pltpu.VMEM((1, width), F32),
            pltpu.VMEM((1, width), F32),
            pltpu.VMEM((1, width), F32),
            pltpu.VMEM((width, width), BF16),
            pltpu.SemaphoreType.DMA((6,)),
            pltpu.SemaphoreType.DMA((CHUNKS,)),
        ],
        cost_estimate=matmul_cost,
        compiler_params=params,
        name="ends",
    )(*map(in_hbm, (events, ids, breaks, gain, rates, keep, in_weight)))

    gate = pl.pallas_call(
        gate_kernel,
        out_shape=sds((rows, width), F32),
        in_specs=[vmem] * 2 + [hbm],
        out_specs=vmem,
        scratch_shapes=[pltpu.VMEM((width, width), BF16), pltpu.SemaphoreType.DMA((CHUNKS,))],
        cost_estimate=matmul_cost,
        compiler_params=params,
        name="gate",
    )(normed, row(out_gain), in_hbm(in_weight))
    level, local = pl.pallas_call(
        functools.partial(local_kernel, users),
        out_shape=(sds((rows, LANES), F32), sds((rows, width), F32)),
        in_specs=[vmem] * 5,
        out_specs=(vmem,) * 2,
        cost_estimate=matmul_cost,
        compiler_params=params,
        name="local",
    )(value, ids, breaks, rates, keep)

    carry = ()
    for index, (axis, stride, size) in enumerate(rounds):
        messages = tuple(
            lax.ppermute(message, axis, shift_pairs(mesh_shape[axis], stride, size, step))
            for step in range(1, size)
        )
        if index == len(rounds) - 1:
            break
        message, totals, counts, *carry = pl.pallas_call(
            functools.partial(merge_kernel, axis, stride, size, index == 0),
            out_shape=(message_type, state_type, counts_type, state_type),
            in_specs=[vmem] * (len(messages) + 4 + len(carry)),
            out_specs=(vmem,) * 4,
            compiler_params=params,
            name="merge",
        )(*messages, totals, counts, *carry, rates, keep)
    return pl.pallas_call(
        functools.partial(final_kernel, axis, stride, size, users),
        out_shape=sds((rows, width), BF16),
        in_specs=[vmem] * (len(messages) + 11),
        out_specs=vmem,
        cost_estimate=matmul_cost,
        compiler_params=params,
        name="final",
    )(
        *messages, totals, counts, *carry, rates, keep, ids, level, local, gate, events, out_weight
    )


def solution(mesh):
    return jax.shard_map(
        functools.partial(on_device, dict(mesh.shape), exchange_rounds(mesh)),
        mesh=mesh,
        in_specs=(P(AXES, None), P(AXES), P(AXES), P(), P(), P(), P(), P(), P()),
        out_specs=P(AXES, None),
        check_vma=False,
    )
```

time: 32.3 us -> 27.8 us (0.86)
  blocking collectives: 15 us -> 0 us
  starting transfers between devices: 2.57 us -> 10.3 us
  waiting for transfers between devices: 2.91 us -> 8.25 us
  Pallas kernels: 11.6 us -> 8.95 us
    all_to_all x1 -> x0, blocking collectives: 15 us -> none  [on_device(): lax.all_to_all(payload.reshape(devices, rows_out, LANES), AXES, split_axi...]
    ppermute x0 -> x5, starting transfers between devices: none -> 10.3 us  [on_device(): lax.ppermute(message, axis, shift_pairs(mesh_shape[axis], stride, size, s...]
    ppermute x0 -> x5, waiting for transfers between devices: none -> 8.25 us  [on_device(): lax.ppermute(message, axis, shift_pairs(mesh_shape[axis], stride, size, s...]
    all_to_all x1 -> x0, waiting for transfers between devices: 2.91 us -> none  [on_device(): lax.all_to_all(carries, AXES, split_axis=0, concat_axis=0, tiled=True)]
    pallas_call x4 -> x8, Pallas kernels: 11.6 us -> 8.95 us  [the longest x1 3.42 us: on_device(): pl.pallas_call(functools.partial(ends_kernel, users), out_shape=(message_...]
    all_to_all x1 -> x0, starting transfers between devices: 2.57 us -> none  [on_device(): lax.all_to_all(carries, AXES, split_axis=0, concat_axis=0, tiled=True)]
  transfers between devices with their start and end apart: 1 -> 5, of which waited for: 1 -> 4; matrix products, arithmetic and copies ran while one was open for 0% -> 0% of each run, Pallas kernels for 13% -> 11%
where the time goes in v3:
time: 27.8 us; the launch traced here: 27.7 us
  starting transfers between devices  10.3 us (37%)
  Pallas kernels  8.95 us (32%)
  waiting for transfers between devices  8.25 us (30%)
    ppermute x5, starting transfers between devices, on_device(): lax.ppermute(message, axis, shift_pairs(mesh_shape[axis], stride, size, s...  10.3 us
    ppermute x5, waiting for transfers between devices, on_device(): lax.ppermute(message, axis, shift_pairs(mesh_shape[axis], stride, size, s...  8.25 us
    pallas_call x1, Pallas kernels, on_device(): pl.pallas_call(functools.partial(ends_kernel, users), out_shape=(message_...  3.42 us
    pallas_call x1, Pallas kernels, on_device(): pl.pallas_call(gate_kernel, out_shape=sds((rows, width), F32), in_specs=[...  2.32 us
    pallas_call x1, Pallas kernels, on_device(): pl.pallas_call(functools.partial(final_kernel, axis, stride, size, users)...  1.56 us
    pallas_call x4, Pallas kernels, on_device(): pl.pallas_call(functools.partial(merge_kernel, axis, stride, size, index...  1.03 us
    pallas_call x1, Pallas kernels, on_device(): pl.pallas_call(functools.partial(local_kernel, users), out_shape=(sds((ro...  0.61 us
  transfers between devices with their start and end apart: 5, of which 4 were waited for; matrix products, arithmetic and copies ran while one was open for 0% of the time, Pallas kernels for 11%

profile of v3, /device:TPU:0, one launch (start us, length us, event | category | flops | bytes accessed | tf_op | source)
XLA Modules:
  0.0 27.7 jit_solution(17790298436396340075)
XLA Ops:
  0.0 0.0 copy-start.2
  0.0 0.0 copy-start.3
  0.0 0.0 copy-start.5
  0.0 0.0 copy-start.6
  0.0 0.0 copy-start.4
  0.0 3.4 %ends.1 = (bf16[32,1152]{1,0:T(8,128)(2,1)S(1)}, f32[32,1024]{1,0:T(8,128)S(1)}, f32[32,128]{1,0:T(8,128)S(1)}, bf16[128,1024]{1,0:T(8,128)(2,1)S(1)}, bf16[128,1024]{1,0:T(8,128)(2,1)S(1)}) custom-call(bf16[128,1024]{1,0:T(8,128)(2,1)} %refs_10_.1, s32[1,128]{1,0:T(1,128)} %bitcast.21, s32[1,128]{1,0:T(1,128)} %bitcast.24, f32[1,1024]{1,0:T(1,128)} %bitcast.26, ...), custom_call_target="tpu_custom_call" | custom-call | flops 268435456 | bytes 2097152 | tf_op jit(solution)/shard_map/ends/pallas_call | solution.py:279
  3.4 0.0 copy-start
  3.5 0.0 copy-start.1
  3.5 3.0 %collective-permute-start = (bf16[32,1152]{1,0:T(8,128)(2,1)S(1)}, bf16[32,1152]{1,0:T(8,128)(2,1)S(1)}, u32[]{:S(2)}, u32[]{:S(2)}) collective-permute-start(bf16[32,1152]{1,0:T(8,128)(2,1)S(1)} %get-tuple-element.28), channel_id=1, source_target_pairs={{0,1},{1,0},{2,3},{3,2},{4,5},{5,4},{6,7},{7,6},{8,9},{9,8},{10,11... | collective-permute-start | bytes 221192 | tf_op jit(solution)/shard_map/ppermute | solution.py:325
  6.5 2.3 %collective-permute-done.refs_0_ = bf16[32,1152]{1,0:T(8,128)(2,1)S(1)} collective-permute-done((bf16[32,1152]{1,0:T(8,128)(2,1)S(1)}, bf16[32,1152]{1,0:T(8,128)(2,1)S(1)}, u32[]{:S(2)}, u32[]{:S(2)}) %collective-permute-start) | collective-permute-done | bytes 73760 | tf_op jit(solution)/shard_map/ppermute | solution.py:325
  8.8 0.0 copy-done.2
  8.9 0.0 copy-done.3
  8.9 0.3 merge.4
  9.1 2.2 %collective-permute-start.1 = (bf16[32,1152]{1,0:T(8,128)(2,1)S(1)}, bf16[32,1152]{1,0:T(8,128)(2,1)S(1)}, u32[]{:S(2)}, u32[]{:S(2)}) collective-permute-start(bf16[32,1152]{1,0:T(8,128)(2,1)S(1)} %get-tuple-element.31), channel_id=1, source_target_pairs={{0,2},{1,3},{2,0},{3,1},{4,6},{5,7},{6,4},{7,5},{8,10},{9,11},{10,... | collective-permute-start | bytes 221192 | tf_op jit(solution)/shard_map/ppermute | solution.py:325
  11.3 2.3 %collective-permute-done.1.refs_0_ = bf16[32,1152]{1,0:T(8,128)(2,1)S(1)} collective-permute-done((bf16[32,1152]{1,0:T(8,128)(2,1)S(1)}, bf16[32,1152]{1,0:T(8,128)(2,1)S(1)}, u32[]{:S(2)}, u32[]{:S(2)}) %collective-permute-start.1) | collective-permute-done | bytes 73760 | tf_op jit(solution)/shard_map/ppermute | solution.py:325
  13.6 0.3 merge.5
  13.9 3.1 %collective-permute-start.2 = (bf16[32,1152]{1,0:T(8,128)(2,1)S(1)}, bf16[32,1152]{1,0:T(8,128)(2,1)S(1)}, u32[]{:S(2)}, u32[]{:S(2)}) collective-permute-start(bf16[32,1152]{1,0:T(8,128)(2,1)S(1)} %get-tuple-element.35), channel_id=1, source_target_pairs={{0,4},{1,5},{2,6},{3,7},{4,0},{5,1},{6,2},{7,3},{8,12},{9,13},{10,... | collective-permute-start | bytes 221192 | tf_op jit(solution)/shard_map/ppermute | solution.py:325
  17.0 2.3 %collective-permute-done.2.refs_0_ = bf16[32,1152]{1,0:T(8,128)(2,1)S(1)} collective-permute-done((bf16[32,1152]{1,0:T(8,128)(2,1)S(1)}, bf16[32,1152]{1,0:T(8,128)(2,1)S(1)}, u32[]{:S(2)}, u32[]{:S(2)}) %collective-permute-start.2) | collective-permute-done | bytes 73760 | tf_op jit(solution)/shard_map/ppermute | solution.py:325
  19.3 0.3 merge.6
  19.6 0.1 collective-permute-start.3
  19.7 1.3 %collective-permute-done.3.refs_0_ = bf16[32,1152]{1,0:T(8,128)(2,1)S(1)} collective-permute-done((bf16[32,1152]{1,0:T(8,128)(2,1)S(1)}, bf16[32,1152]{1,0:T(8,128)(2,1)S(1)}, u32[]{:S(2)}, u32[]{:S(2)}) %collective-permute-start.3) | collective-permute-done | bytes 73760 | tf_op jit(solution)/shard_map/ppermute | solution.py:325
  20.9 0.3 merge.7
  21.2 1.9 %collective-permute-start.4 = (bf16[32,1152]{1,0:T(8,128)(2,1)S(1)}, bf16[32,1152]{1,0:T(8,128)(2,1)S(1)}, u32[]{:S(2)}, u32[]{:S(2)}) collective-permute-start(bf16[32,1152]{1,0:T(8,128)(2,1)S(1)} %get-tuple-element.43), channel_id=1, source_target_pairs={{0,16},{8,24},{16,0},{24,8},{1,17},{9,25},{17,1},{25,9},{2,18},{10... | collective-permute-start | bytes 221192 | tf_op jit(solution)/shard_map/ppermute | solution.py:325
  23.1 0.0 copy-done.5
  23.1 0.0 copy-done.6
  23.1 0.6 %local.1 = (f32[128,128]{1,0:T(8,128)S(1)}, f32[128,1024]{1,0:T(8,128)S(1)}) custom-call(bf16[128,1024]{1,0:T(8,128)(2,1)S(1)} %get-tuple-element.47.value, s32[1,128]{1,0:T(1,128)S(1)} %bitcast.22, s32[1,128]{1,0:T(1,128)S(1)} %bitcast.25, f32[1,1024]{1,0:T(1,128)S(1)} %bitcast.11, f32[1,1024]{1,0:T(1,128)S(1)} %bitcast.18), custom_call_target="tpu_custom_call" | custom-call | flops 268435456 | bytes 2097152 | tf_op jit(solution)/shard_map/local/pallas_call | solution.py:312
  23.7 0.0 copy-done.4
  23.7 2.3 %gate.1.refs_9_ = f32[128,1024]{1,0:T(8,128)S(1)} custom-call(bf16[128,1024]{1,0:T(8,128)(2,1)S(1)} %get-tuple-element.50.normed, f32[1,1024]{1,0:T(1,128)S(1)} %bitcast.20, bf16[1024,2048]{1,0:T(8,128)(2,1)} %weight_hbm.3), custom_call_target="tpu_custom_call" | custom-call | flops 268435456 | bytes 2097152 | tf_op jit(solution)/shard_map/gate/pallas_call | solution.py:302
  26.1 0.0 collective-permute-done.4.refs_0_
  26.1 0.0 copy-done
  26.1 0.0 copy-done.1
  26.1 1.6 %final.1 = bf16[128,1024]{1,0:T(8,128)(2,1)} custom-call(bf16[32,1152]{1,0:T(8,128)(2,1)S(1)} %collective-permute-done.4.refs_0_, f32[32,1024]{1,0:T(8,128)S(1)} %get-tuple-element.44.refs_1_, f32[32,128]{1,0:T(8,128)S(1)} %get-tuple-element.45.refs_2_, f32[32,1024]{1,0:T(8,128)S(1)} %get-tuple-element.46.refs_3_, f32[1,1024]{1,0:T(1,128)S(1)} %bitcast.12, ...), custom_call_target="tpu_custom_call" | custom-call | flops 268435456 | bytes 2097152 | tf_op jit(solution)/shard_map/final/pallas_call | solution.py:338
Async XLA Ops:
  0.0 8.9 %copy-start.2 = (f32[1024]{0:T(1024)S(1)}, f32[1024]{0:T(1024)}, u32[]{:S(2)}) copy-start(f32[1024]{0:T(1024)} %param.14) | copy-start | bytes 12292
  0.0 8.9 %copy-start.3 = (f32[1024]{0:T(1024)S(1)}, f32[1024]{0:T(1024)}, u32[]{:S(2)}) copy-start(f32[1024]{0:T(1024)} %param.15) | copy-start | bytes 12292
  0.0 23.1 %copy-start.5 = (s32[128]{0:T(128)S(1)}, s32[128]{0:T(128)}, u32[]{:S(2)}) copy-start(s32[128]{0:T(128)} %param.10) | copy-start | bytes 1540
  0.0 23.1 %copy-start.6 = (s32[128]{0:T(128)S(1)}, s32[128]{0:T(128)}, u32[]{:S(2)}) copy-start(s32[128]{0:T(128)} %param.11) | copy-start | bytes 1540
  0.0 23.7 %copy-start.4 = (f32[1024]{0:T(1024)S(1)}, f32[1024]{0:T(1024)}, u32[]{:S(2)}) copy-start(f32[1024]{0:T(1024)} %param.16) | copy-start | bytes 12292
  3.4 22.6 %copy-start = (bf16[1024,1024]{1,0:T(8,128)(2,1)S(1)}, bf16[1024,1024]{1,0:T(8,128)(2,1)}, u32[]{:S(2)}) copy-start(bf16[1024,1024]{1,0:T(8,128)(2,1)} %refs_11_.1) | copy-start | bytes 6291460
  3.5 22.6 %copy-start.1 = (bf16[128,1024]{1,0:T(8,128)(2,1)S(1)}, bf16[128,1024]{1,0:T(8,128)(2,1)}, u32[]{:S(2)}) copy-start(bf16[128,1024]{1,0:T(8,128)(2,1)} %refs_10_.1) | copy-start | bytes 786436
  3.5 5.4 %collective-permute-start = (bf16[32,1152]{1,0:T(8,128)(2,1)S(1)}, bf16[32,1152]{1,0:T(8,128)(2,1)S(1)}, u32[]{:S(2)}, u32[]{:S(2)}) collective-permute-start(bf16[32,1152]{1,0:T(8,128)(2,1)S(1)} %get-tuple-element.28), channel_id=1, source_target_pairs={{0,1},{1,0},{2,3},{3,2},{4,5},{5,4},{6,7},{7,6},{8,9},{9,8},{10,11... | collective-permute-start | bytes 221192 | tf_op jit(solution)/shard_map/ppermute | solution.py:325
  9.1 4.5 %collective-permute-start.1 = (bf16[32,1152]{1,0:T(8,128)(2,1)S(1)}, bf16[32,1152]{1,0:T(8,128)(2,1)S(1)}, u32[]{:S(2)}, u32[]{:S(2)}) collective-permute-start(bf16[32,1152]{1,0:T(8,128)(2,1)S(1)} %get-tuple-element.31), channel_id=1, source_target_pairs={{0,2},{1,3},{2,0},{3,1},{4,6},{5,7},{6,4},{7,5},{8,10},{9,11},{10,... | collective-permute-start | bytes 221192 | tf_op jit(solution)/shard_map/ppermute | solution.py:325
  13.9 5.4 %collective-permute-start.2 = (bf16[32,1152]{1,0:T(8,128)(2,1)S(1)}, bf16[32,1152]{1,0:T(8,128)(2,1)S(1)}, u32[]{:S(2)}, u32[]{:S(2)}) collective-permute-start(bf16[32,1152]{1,0:T(8,128)(2,1)S(1)} %get-tuple-element.35), channel_id=1, source_target_pairs={{0,4},{1,5},{2,6},{3,7},{4,0},{5,1},{6,2},{7,3},{8,12},{9,13},{10,... | collective-permute-start | bytes 221192 | tf_op jit(solution)/shard_map/ppermute | solution.py:325
  19.6 1.3 %collective-permute-start.3 = (bf16[32,1152]{1,0:T(8,128)(2,1)S(1)}, bf16[32,1152]{1,0:T(8,128)(2,1)S(1)}, u32[]{:S(2)}, u32[]{:S(2)}) collective-permute-start(bf16[32,1152]{1,0:T(8,128)(2,1)S(1)} %get-tuple-element.39), channel_id=1, source_target_pairs={{0,8},{8,0},{16,24},{24,16},{1,9},{9,1},{17,25},{25,17},{2,10},{10... | collective-permute-start | bytes 221192 | tf_op jit(solution)/shard_map/ppermute | solution.py:325
  21.2 4.9 %collective-permute-start.4 = (bf16[32,1152]{1,0:T(8,128)(2,1)S(1)}, bf16[32,1152]{1,0:T(8,128)(2,1)S(1)}, u32[]{:S(2)}, u32[]{:S(2)}) collective-permute-start(bf16[32,1152]{1,0:T(8,128)(2,1)S(1)} %get-tuple-element.43), channel_id=1, source_target_pairs={{0,16},{8,24},{16,0},{24,8},{1,17},{9,25},{17,1},{25,9},{2,18},{10... | collective-permute-start | bytes 221192 | tf_op jit(solution)/shard_map/ppermute | solution.py:325

commit v4 on v3

v4 whole, which is shorter than its diff:
```python
import functools

import jax
import jax.numpy as jnp
from jax import lax
from jax.experimental import pallas as pl
from jax.experimental.pallas import tpu as pltpu
from jax.sharding import PartitionSpec as P

U_DEV = 4
LANES = 128
CHUNKS = 4
GATE_ROUND = 2
SPLIT = (1, 1)
RADIX = 128.0
LOG2_E = 1.4426950408889634
VMEM_BYTES = 12 * 2**20
AXES = ("grp", "shard")
F32, BF16 = jnp.float32, jnp.bfloat16


def dot(left, right):
    return jnp.dot(left, right, preferred_element_type=F32)


def dot_t(left, right):
    return lax.dot_general(left, right, (((0,), (0,)), ((), ())), preferred_element_type=F32)


def rms_rows(values):
    return lax.rsqrt(jnp.mean(values * values, axis=-1, keepdims=True) + 1e-06)


def member_rows(ids_row, users):
    user = lax.broadcasted_iota(jnp.int32, (users, ids_row.shape[1]), 0)
    return (user == ids_row).astype(F32)


def row_compare(rows, compare):
    square = (rows, rows)
    return compare(
        lax.broadcasted_iota(jnp.int32, square, 1), lax.broadcasted_iota(jnp.int32, square, 0)
    )


def as_lanes(columns):
    shape = (columns[0].shape[0], LANES)
    lane = lax.broadcasted_iota(jnp.int32, shape, 1)
    total = jnp.zeros(shape, F32)
    for i, column in enumerate(columns):
        total = jnp.where(lane == i, column, total)
    return total


def started(copies):
    for copy in copies:
        copy.start()
    return copies


def column_spans(width, split):
    unit, spans, start = width // sum(split), [], 0
    for share in split:
        spans.append(pl.ds(start, share * unit))
        start += share * unit
    return spans


def weight_copies(hbm, vmem, sem, spans, first):
    return [
        pltpu.make_async_copy(
            hbm.at[:, pl.ds(first + span.start, span.size)], vmem.at[:, span], sem.at[c]
        )
        for c, span in enumerate(spans)
    ]


def write_counts(message, events, breaks):
    width = message.shape[1] - LANES
    high_events = jnp.floor(events * (1.0 / RADIX))
    high_breaks = jnp.floor(breaks * (1.0 / RADIX))
    message[:, width:] = as_lanes(
        [high_events, events - RADIX * high_events, high_breaks, breaks - RADIX * high_breaks]
    ).astype(BF16)


def fade(levels, cols, events, breaks):
    return jnp.exp2(levels[0:1, cols] * events + levels[1:2, cols] * breaks)


def ends_kernel(
    users,
    events_hbm, ids_hbm, breaks_hbm, in_gain_hbm, rates_hbm, keep_hbm, weight_hbm,
    message, totals, counts, levels, normed_out, value_out,
    events, ids, breaks, in_gain, rates, keep, held, small_sem, sem,
):
    rows, width = events.shape
    small = started(
        [
            pltpu.make_async_copy(source, target, small_sem.at[i])
            for i, (source, target) in enumerate(
                (
                    (ids_hbm, ids),
                    (breaks_hbm, breaks),
                    (rates_hbm, rates),
                    (keep_hbm, keep),
                    (events_hbm, events),
                    (in_gain_hbm, in_gain),
                )
            )
        ]
    )
    spans = column_spans(width, SPLIT)
    copies = started(weight_copies(weight_hbm, held, sem, spans, width))
    for copy in small[:4]:
        copy.wait()
    break_row = breaks[...].astype(F32)
    member = member_rows(ids[...], users)
    member_b = member.astype(BF16)
    later = jnp.where(row_compare(rows, jnp.greater), dot_t(member_b, member_b), 0.0)
    events_left = jnp.sum(later, axis=1, keepdims=True)
    breaks_left = jnp.sum(later * break_row, axis=1, keepdims=True)
    user_events = jnp.sum(member, axis=1, keepdims=True)
    user_breaks = jnp.sum(member * break_row, axis=1, keepdims=True)
    counts[...] = as_lanes([user_events, user_breaks])
    levels[0:1, :] = rates[...] * -LOG2_E
    levels[1:2, :] = jnp.log(keep[...]) * LOG2_E
    write_counts(message, user_events, user_breaks)
    for copy in small[4:]:
        copy.wait()
    event_rows = events[...].astype(F32)
    normed = (event_rows * rms_rows(event_rows) * in_gain[...]).astype(BF16)
    normed_out[...] = normed
    previous = None
    for c in range(len(spans) + 1):
        latest = None
        if c < len(spans):
            copies[c].wait()
            value = dot(normed, held[:, spans[c]]).astype(BF16)
            value_out[:, spans[c]] = value
            latest = value, fade(levels, spans[c], events_left, breaks_left)
        if c > 0:
            value, faded = previous
            ends = dot(member_b, (faded * value.astype(F32)).astype(BF16))
            totals[:, spans[c - 1]] = ends
            message[:, spans[c - 1]] = ends.astype(BF16)
        previous = latest


def gate_kernel(normed, out_gain, _, weight_hbm, gate_out, done, held, sem):
    width = normed.shape[1]
    spans = column_spans(width, SPLIT)
    copies = started(weight_copies(weight_hbm, held, sem, spans, 0))
    for copy, cols in zip(copies, spans):
        copy.wait()
        gate = dot(normed[...], held[:, cols]).astype(BF16).astype(F32)
        gate_out[:, cols] = out_gain[:, cols] * (gate / (1.0 + jnp.exp(-gate)))
    done[...] = jnp.zeros_like(done)


def local_kernel(users, value, ids, breaks, levels, growth_out, local_out):
    rows, width = value.shape
    break_row = breaks[...].astype(F32)
    member_b = member_rows(ids[...], users).astype(BF16)
    within = jnp.where(row_compare(rows, jnp.less_equal), dot_t(member_b, member_b), 0.0)
    count = jnp.sum(within, axis=1, keepdims=True)
    count_breaks = jnp.sum(within * break_row, axis=1, keepdims=True)
    within_b = within.astype(BF16)
    within_twice = jnp.concatenate([within_b, within_b], axis=1)
    scaled = fade(levels, slice(None), -count, -count_breaks) * value[...].astype(F32)
    high = scaled.astype(BF16)
    low = (scaled - high.astype(F32)).astype(BF16)
    growth = fade(levels, slice(None), count, count_breaks)
    growth_out[...] = growth
    local_out[...] = growth * dot(within_twice, jnp.concatenate([high, low], axis=0))


def received(message):
    got = message[...].astype(F32)
    sums, digits = got[:, :-LANES], got[:, -LANES:]
    column = lambda i: digits[:, i:i + 1]
    return sums, RADIX * column(0) + column(1), RADIX * column(2) + column(3)


def joined(levels, first, second):
    if first is None or second is None:
        return second if first is None else first
    return (
        fade(levels, slice(None), second[1], second[2]) * first[0] + second[0],
        first[1] + second[1],
        first[2] + second[2],
    )


def place_of(axis, stride, size):
    return lax.rem(lax.div(lax.axis_index(axis), stride), size)


def merge_kernel(axis, stride, size, fresh, *refs):
    messages, (totals, counts, *rest) = refs[:size - 1], refs[size - 1:]
    carry_in = None if fresh else rest.pop(0)
    levels, _, message, counts_out, carry_out, *totals_out = rest

    def folded(place):
        column = lambda i: counts[:, i:i + 1]
        own = (totals[...], column(0), column(1))
        carry = None if fresh else (carry_in[...], column(2), column(3))
        blocks = [received(ref) for ref in messages]
        for block in blocks[:place]:
            carry = joined(levels, block, carry)
            own = joined(levels, block, own)
        for block in reversed(blocks[place:]):
            own = joined(levels, own, block)
        if carry is None:
            carry = (jnp.zeros_like(own[0]), jnp.zeros_like(own[1]), jnp.zeros_like(own[2]))
        message[:, :totals.shape[1]] = own[0].astype(BF16)
        write_counts(message, own[1], own[2])
        if totals_out:
            totals_out[0][...] = own[0]
        counts_out[...] = as_lanes([own[1], own[2], carry[1], carry[2]])
        carry_out[...] = carry[0]

    for place in range(size):
        pl.when(place_of(axis, stride, size) == place)(functools.partial(folded, place))


def final_kernel(axis, stride, size, users, *refs):
    messages, rest = refs[:size - 1], refs[size - 1:]
    counts, carry, levels, ids, growth, local, gate, events, weight, out_hbm, out, sem = rest
    width = events.shape[1]
    place = place_of(axis, stride, size)
    block = (carry[...], counts[:, 2:3], counts[:, 3:4])
    for m, message in enumerate(messages, 1):
        block = joined(levels, [jnp.where(place >= m, a, 0.0) for a in received(message)], block)
    high = block[0].astype(BF16)
    low = (block[0] - high.astype(F32)).astype(BF16)
    member_b = member_rows(ids[...], users).astype(BF16)
    entering = dot_t(
        jnp.concatenate([member_b, member_b], axis=0), jnp.concatenate([high, low], axis=0)
    )
    hidden = local[...] + growth[...] * entering
    mixed_part = (hidden * rms_rows(hidden) * gate[...]).astype(BF16)
    copies = []
    for c, cols in enumerate(column_spans(width, (1,) * CHUNKS)):
        out[:, cols] = (events[:, cols].astype(F32) + dot(mixed_part, weight[:, cols])).astype(BF16)
        copies.append(pltpu.make_async_copy(out.at[:, cols], out_hbm.at[:, cols], sem.at[c]))
        copies[c].start()
    for copy in copies:
        copy.wait()


def exchange_rounds(mesh):
    rounds = []
    for axis in reversed(AXES):
        stride, left = 1, mesh.shape[axis]
        for size in range(2, left + 1):
            while left % size == 0:
                rounds.append((axis, stride, size))
                stride, left = stride * size, left // size
    return rounds


def exchange_pairs(length, stride, size, step):
    pairs = []
    for source in range(length):
        place = source // stride % size
        target = (place + step) % size
        pairs.append((source, source + (target - place) * stride))
    return pairs


def on_device(
    mesh_shape,
    rounds,
    events,
    user_ids,
    session_break,
    in_gain,
    in_weight,
    decay_rates,
    keep_factor,
    out_gain,
    out_weight,
):
    rows, width = events.shape
    users = U_DEV * mesh_shape["shard"]
    ids = user_ids.reshape(1, rows)
    breaks = session_break.reshape(1, rows)
    row = lambda vector: vector.reshape(1, width)
    gain, rates, keep = row(in_gain), row(decay_rates), row(keep_factor)
    hbm = pl.BlockSpec(memory_space=pltpu.HBM)
    vmem = pl.BlockSpec(memory_space=pltpu.VMEM)
    in_hbm = lambda value: pltpu.with_memory_space_constraint(value, pltpu.HBM)
    sds = jax.ShapeDtypeStruct
    params = pltpu.CompilerParams(vmem_limit_bytes=VMEM_BYTES)
    matmul_cost = pl.CostEstimate(
        flops=2 * rows * width * width, bytes_accessed=2 * width * width, transcendentals=0
    )
    message_type = sds((users, width + LANES), BF16)
    state_type = sds((users, width), F32)
    counts_type = sds((users, LANES), F32)

    message, totals, counts, levels, normed, value = pl.pallas_call(
        functools.partial(ends_kernel, users),
        out_shape=(
            message_type, state_type, counts_type, sds((2, width), F32),
            sds((rows, width), BF16), sds((rows, width), BF16),
        ),
        in_specs=[hbm] * 7,
        out_specs=(vmem,) * 6,
        scratch_shapes=[
            pltpu.VMEM((rows, width), BF16),
            pltpu.VMEM((1, rows), jnp.int32),
            pltpu.VMEM((1, rows), jnp.int32),
            pltpu.VMEM((1, width), F32),
            pltpu.VMEM((1, width), F32),
            pltpu.VMEM((1, width), F32),
            pltpu.VMEM((width, width), BF16),
            pltpu.SemaphoreType.DMA((6,)),
            pltpu.SemaphoreType.DMA((len(SPLIT),)),
        ],
        cost_estimate=matmul_cost,
        compiler_params=params,
        name="ends",
    )(*map(in_hbm, (events, ids, breaks, gain, rates, keep, in_weight)))
    growth, local = pl.pallas_call(
        functools.partial(local_kernel, users),
        out_shape=(sds((rows, width), F32),) * 2,
        in_specs=[vmem] * 4,
        out_specs=(vmem,) * 2,
        cost_estimate=matmul_cost,
        compiler_params=params,
        name="local",
    )(value, ids, breaks, levels)

    carry = ()
    done = counts
    last = len(rounds) - 1
    for index, (axis, stride, size) in enumerate(rounds):
        messages = tuple(
            lax.ppermute(message, axis, exchange_pairs(mesh_shape[axis], stride, size, step))
            for step in range(1, size)
        )
        if index == GATE_ROUND:
            gate, done = pl.pallas_call(
                gate_kernel,
                out_shape=(sds((rows, width), F32), sds((8, LANES), F32)),
                in_specs=[vmem] * 3 + [hbm],
                out_specs=(vmem, vmem),
                scratch_shapes=[
                    pltpu.VMEM((width, width), BF16), pltpu.SemaphoreType.DMA((len(SPLIT),))
                ],
                cost_estimate=matmul_cost,
                compiler_params=params,
                name="gate",
            )(normed, row(out_gain), counts, in_hbm(in_weight))
        if index == last:
            break
        out_types = (message_type, counts_type, state_type) + (state_type,) * (index + 1 < last)
        message, counts, *state = pl.pallas_call(
            functools.partial(merge_kernel, axis, stride, size, index == 0),
            out_shape=out_types,
            in_specs=[vmem] * (len(messages) + 4 + len(carry)),
            out_specs=(vmem,) * len(out_types),
            compiler_params=params,
            name="merge",
        )(*messages, totals, counts, *carry, levels, done)
        carry, totals, done = state[:1], state[-1], counts
    return pl.pallas_call(
        functools.partial(final_kernel, axis, stride, size, users),
        out_shape=sds((rows, width), BF16),
        in_specs=[vmem] * (len(messages) + 9),
        out_specs=hbm,
        scratch_shapes=[pltpu.VMEM((rows, width), BF16), pltpu.SemaphoreType.DMA((CHUNKS,))],
        cost_estimate=matmul_cost,
        compiler_params=params,
        name="final",
    )(*messages, counts, *carry, levels, ids, growth, local, gate, events, out_weight)


def solution(mesh):
    return jax.shard_map(
        functools.partial(on_device, dict(mesh.shape), exchange_rounds(mesh)),
        mesh=mesh,
        in_specs=(P(AXES, None), P(AXES), P(AXES), P(), P(), P(), P(), P(), P()),
        out_specs=P(AXES, None),
        check_vma=False,
    )
```

time: 27.8 us -> 26.1 us (0.939)
  Pallas kernels: 8.95 us -> 7.3 us
    pallas_call x1, Pallas kernels: 3.42 us -> 2.24 us  [on_device(): pl.pallas_call(functools.partial(ends_kernel, users), out_shape=(message_...]
    pallas_call x1, Pallas kernels: 2.32 us -> 2.01 us  [on_device(): pl.pallas_call(gate_kernel, out_shape=(sds((rows, width), F32), sds((8, L...]
  transfers between devices with their start and end apart: 5 -> 5, of which waited for: 4 -> 5; matrix products, arithmetic and copies ran while one was open for 0% -> 0% of each run, Pallas kernels for 11% -> 10%
where the time goes in v4:
time: 26.1 us; the launch traced here: 25.9 us
  starting transfers between devices  10.3 us (39%)
  waiting for transfers between devices  8.2 us (31%)
  Pallas kernels  7.3 us (28%)
    ppermute x5, starting transfers between devices, on_device(): lax.ppermute(message, axis, exchange_pairs(mesh_shape[axis], stride, size...  10.3 us
    ppermute x5, waiting for transfers between devices, on_device(): lax.ppermute(message, axis, exchange_pairs(mesh_shape[axis], stride, size...  8.2 us
    pallas_call x1, Pallas kernels, on_device(): pl.pallas_call(functools.partial(ends_kernel, users), out_shape=(message_...  2.24 us
    pallas_call x1, Pallas kernels, on_device(): pl.pallas_call(gate_kernel, out_shape=(sds((rows, width), F32), sds((8, L...  2.01 us
    pallas_call x1, Pallas kernels, on_device(): pl.pallas_call(functools.partial(final_kernel, axis, stride, size, users)...  1.5 us
    pallas_call x4, Pallas kernels, on_device(): pl.pallas_call(functools.partial(merge_kernel, axis, stride, size, index...  0.95 us
    pallas_call x1, Pallas kernels, on_device(): pl.pallas_call(functools.partial(local_kernel, users), out_shape=(sds((ro...  0.59 us
  transfers between devices with their start and end apart: 5, of which 5 were waited for; matrix products, arithmetic and copies ran while one was open for 0% of the time, Pallas kernels for 10%

profile of v4, /device:TPU:0, one launch (start us, length us, event | category | flops | bytes accessed | tf_op | source)
XLA Modules:
  0.0 25.9 jit_solution(17694658462052604711)
XLA Ops:
  0.0 0.0 copy-start.2
  0.0 0.0 copy-start.3
  0.0 0.0 copy-start.4
  0.0 2.2 %ends.1 = (bf16[32,1152]{1,0:T(8,128)(2,1)S(1)}, f32[32,1024]{1,0:T(8,128)S(1)}, f32[32,128]{1,0:T(8,128)S(1)}, f32[2,1024]{1,0:T(2,128)S(1)}, bf16[128,1024]{1,...) custom-call(bf16[128,1024]{1,0:T(8,128)(2,1)} %refs_8_.1, s32[1,128]{1,0:T(1,128)} %bitcast.7, s32[1,128]{1,0:T(1,128)} %bitcast.10, ...), custom_call_target="tpu_custom_call" | custom-call | flops 268435456 | bytes 2097152 | tf_op jit(solution)/shard_map/ends/pallas_call | solution.py:303
  2.3 0.0 copy-start
  2.3 0.0 copy-start.1
  2.3 3.0 %collective-permute-start = (bf16[32,1152]{1,0:T(8,128)(2,1)S(1)}, bf16[32,1152]{1,0:T(8,128)(2,1)S(1)}, u32[]{:S(2)}, u32[]{:S(2)}) collective-permute-start(bf16[32,1152]{1,0:T(8,128)(2,1)S(1)} %get-tuple-element.30), channel_id=1, source_target_pairs={{0,1},{1,0},{2,3},{3,2},{4,5},{5,4},{6,7},{7,6},{8,9},{9,8},{10,11... | collective-permute-start | bytes 221192 | tf_op jit(solution)/shard_map/ppermute | solution.py:341
  5.3 2.3 %collective-permute-done.refs_0_ = bf16[32,1152]{1,0:T(8,128)(2,1)S(1)} collective-permute-done((bf16[32,1152]{1,0:T(8,128)(2,1)S(1)}, bf16[32,1152]{1,0:T(8,128)(2,1)S(1)}, u32[]{:S(2)}, u32[]{:S(2)}) %collective-permute-start) | collective-permute-done | bytes 73760 | tf_op jit(solution)/shard_map/ppermute | solution.py:341
  7.6 0.2 merge.4
  7.9 2.2 %collective-permute-start.1 = (bf16[32,1152]{1,0:T(8,128)(2,1)S(1)}, bf16[32,1152]{1,0:T(8,128)(2,1)S(1)}, u32[]{:S(2)}, u32[]{:S(2)}) collective-permute-start(bf16[32,1152]{1,0:T(8,128)(2,1)S(1)} %get-tuple-element.34), channel_id=1, source_target_pairs={{0,2},{1,3},{2,0},{3,1},{4,6},{5,7},{6,4},{7,5},{8,10},{9,11},{10,... | collective-permute-start | bytes 221192 | tf_op jit(solution)/shard_map/ppermute | solution.py:341
  10.0 2.3 %collective-permute-done.1.refs_0_ = bf16[32,1152]{1,0:T(8,128)(2,1)S(1)} collective-permute-done((bf16[32,1152]{1,0:T(8,128)(2,1)S(1)}, bf16[32,1152]{1,0:T(8,128)(2,1)S(1)}, u32[]{:S(2)}, u32[]{:S(2)}) %collective-permute-start.1) | collective-permute-done | bytes 73760 | tf_op jit(solution)/shard_map/ppermute | solution.py:341
  12.4 0.2 merge.5
  12.6 3.1 %collective-permute-start.2 = (bf16[32,1152]{1,0:T(8,128)(2,1)S(1)}, bf16[32,1152]{1,0:T(8,128)(2,1)S(1)}, u32[]{:S(2)}, u32[]{:S(2)}) collective-permute-start(bf16[32,1152]{1,0:T(8,128)(2,1)S(1)} %get-tuple-element.38), channel_id=1, source_target_pairs={{0,4},{1,5},{2,6},{3,7},{4,0},{5,1},{6,2},{7,3},{8,12},{9,13},{10,... | collective-permute-start | bytes 221192 | tf_op jit(solution)/shard_map/ppermute | solution.py:341
  15.7 0.0 copy-done.2
  15.7 2.0 %gate.1 = (f32[128,1024]{1,0:T(8,128)S(1)}, f32[8,128]{1,0:T(8,128)S(1)}) custom-call(bf16[128,1024]{1,0:T(8,128)(2,1)S(1)} %get-tuple-element.42.normed, f32[1,1024]{1,0:T(1,128)S(1)} %bitcast.6, f32[32,128]{1,0:T(8,128)S(1)} %get-tuple-element.40._.refs_2_, bf16[1024,2048]{1,0:T(8,128)(2,1)} %weight_hbm.3), custom_call_target="tpu_custom_call" | custom-call | flops 268435456 | bytes 2097152 | tf_op jit(solution)/shard_map/gate/pallas_call | solution.py:345
  17.8 0.3 %collective-permute-done.2.refs_0_ = bf16[32,1152]{1,0:T(8,128)(2,1)S(1)} collective-permute-done((bf16[32,1152]{1,0:T(8,128)(2,1)S(1)}, bf16[32,1152]{1,0:T(8,128)(2,1)S(1)}, u32[]{:S(2)}, u32[]{:S(2)}) %collective-permute-start.2) | collective-permute-done | bytes 73760 | tf_op jit(solution)/shard_map/ppermute | solution.py:341
  18.1 0.2 merge.6
  18.3 0.1 collective-permute-start.3
  18.4 1.3 %collective-permute-done.3.refs_0_ = bf16[32,1152]{1,0:T(8,128)(2,1)S(1)} collective-permute-done((bf16[32,1152]{1,0:T(8,128)(2,1)S(1)}, bf16[32,1152]{1,0:T(8,128)(2,1)S(1)}, u32[]{:S(2)}, u32[]{:S(2)}) %collective-permute-start.3) | collective-permute-done | bytes 73760 | tf_op jit(solution)/shard_map/ppermute | solution.py:341
  19.6 0.2 merge.7
  19.9 1.9 %collective-permute-start.4 = (bf16[32,1152]{1,0:T(8,128)(2,1)S(1)}, bf16[32,1152]{1,0:T(8,128)(2,1)S(1)}, u32[]{:S(2)}, u32[]{:S(2)}) collective-permute-start(bf16[32,1152]{1,0:T(8,128)(2,1)S(1)} %get-tuple-element.48), channel_id=1, source_target_pairs={{0,16},{8,24},{16,0},{24,8},{1,17},{9,25},{17,1},{25,9},{2,18},{10... | collective-permute-start | bytes 221192 | tf_op jit(solution)/shard_map/ppermute | solution.py:341
  21.8 0.0 copy-done.3
  21.8 0.0 copy-done.4
  21.8 0.6 %local.1 = (f32[128,1024]{1,0:T(8,128)S(1)}, f32[128,1024]{1,0:T(8,128)S(1)}) custom-call(bf16[128,1024]{1,0:T(8,128)(2,1)S(1)} %get-tuple-element.51.value, s32[1,128]{1,0:T(1,128)S(1)} %bitcast.8, s32[1,128]{1,0:T(1,128)S(1)} %bitcast.11, f32[2,1024]{1,0:T(2,128)S(1)} %get-tuple-element.33.refs_3_.refs_4_.levels), custom_call_target="tpu_custom_call" | custom-call | flops 268435456 | bytes 2097152 | tf_op jit(solution)/shard_map/local/pallas_call | solution.py:326
  22.4 2.0 %collective-permute-done.4.refs_0_ = bf16[32,1152]{1,0:T(8,128)(2,1)S(1)} collective-permute-done((bf16[32,1152]{1,0:T(8,128)(2,1)S(1)}, bf16[32,1152]{1,0:T(8,128)(2,1)S(1)}, u32[]{:S(2)}, u32[]{:S(2)}) %collective-permute-start.4) | collective-permute-done | bytes 73760 | tf_op jit(solution)/shard_map/ppermute | solution.py:341
  24.4 0.0 copy-done
  24.4 0.0 copy-done.1
  24.4 1.5 %final.1 = bf16[128,1024]{1,0:T(8,128)(2,1)} custom-call(bf16[32,1152]{1,0:T(8,128)(2,1)S(1)} %collective-permute-done.4.refs_0_, f32[32,128]{1,0:T(8,128)S(1)} %get-tuple-element.49.refs_1_, f32[32,1024]{1,0:T(8,128)S(1)} %get-tuple-element.50.refs_2_, f32[2,1024]{1,0:T(2,128)S(1)} %get-tuple-element.33.refs_3_.refs_4_.levels, s32[1,128]{1,0:T(1,128)S(1)} %bitcast.9, ...), custom_call_target="tpu_custom_call" | custom-call | flops 268435456 | bytes 2097152 | tf_op jit(solution)/shard_map/final/pallas_call | solution.py:369
Async XLA Ops:
  0.0 15.7 %copy-start.2 = (f32[1024]{0:T(1024)S(1)}, f32[1024]{0:T(1024)}, u32[]{:S(2)}) copy-start(f32[1024]{0:T(1024)} %param.16) | copy-start | bytes 12292
  0.0 21.8 %copy-start.3 = (s32[128]{0:T(128)S(1)}, s32[128]{0:T(128)}, u32[]{:S(2)}) copy-start(s32[128]{0:T(128)} %param.10) | copy-start | bytes 1540
  0.0 21.8 %copy-start.4 = (s32[128]{0:T(128)S(1)}, s32[128]{0:T(128)}, u32[]{:S(2)}) copy-start(s32[128]{0:T(128)} %param.11) | copy-start | bytes 1540
  2.3 22.1 %copy-start = (bf16[1024,1024]{1,0:T(8,128)(2,1)S(1)}, bf16[1024,1024]{1,0:T(8,128)(2,1)}, u32[]{:S(2)}) copy-start(bf16[1024,1024]{1,0:T(8,128)(2,1)} %refs_9_.1) | copy-start | bytes 6291460
  2.3 22.1 %copy-start.1 = (bf16[128,1024]{1,0:T(8,128)(2,1)S(1)}, bf16[128,1024]{1,0:T(8,128)(2,1)}, u32[]{:S(2)}) copy-start(bf16[128,1024]{1,0:T(8,128)(2,1)} %refs_8_.1) | copy-start | bytes 786436
  2.3 5.4 %collective-permute-start = (bf16[32,1152]{1,0:T(8,128)(2,1)S(1)}, bf16[32,1152]{1,0:T(8,128)(2,1)S(1)}, u32[]{:S(2)}, u32[]{:S(2)}) collective-permute-start(bf16[32,1152]{1,0:T(8,128)(2,1)S(1)} %get-tuple-element.30), channel_id=1, source_target_pairs={{0,1},{1,0},{2,3},{3,2},{4,5},{5,4},{6,7},{7,6},{8,9},{9,8},{10,11... | collective-permute-start | bytes 221192 | tf_op jit(solution)/shard_map/ppermute | solution.py:341
  7.9 4.5 %collective-permute-start.1 = (bf16[32,1152]{1,0:T(8,128)(2,1)S(1)}, bf16[32,1152]{1,0:T(8,128)(2,1)S(1)}, u32[]{:S(2)}, u32[]{:S(2)}) collective-permute-start(bf16[32,1152]{1,0:T(8,128)(2,1)S(1)} %get-tuple-element.34), channel_id=1, source_target_pairs={{0,2},{1,3},{2,0},{3,1},{4,6},{5,7},{6,4},{7,5},{8,10},{9,11},{10,... | collective-permute-start | bytes 221192 | tf_op jit(solution)/shard_map/ppermute | solution.py:341
  12.6 5.4 %collective-permute-start.2 = (bf16[32,1152]{1,0:T(8,128)(2,1)S(1)}, bf16[32,1152]{1,0:T(8,128)(2,1)S(1)}, u32[]{:S(2)}, u32[]{:S(2)}) collective-permute-start(bf16[32,1152]{1,0:T(8,128)(2,1)S(1)} %get-tuple-element.38), channel_id=1, source_target_pairs={{0,4},{1,5},{2,6},{3,7},{4,0},{5,1},{6,2},{7,3},{8,12},{9,13},{10,... | collective-permute-start | bytes 221192 | tf_op jit(solution)/shard_map/ppermute | solution.py:341
  18.3 1.3 %collective-permute-start.3 = (bf16[32,1152]{1,0:T(8,128)(2,1)S(1)}, bf16[32,1152]{1,0:T(8,128)(2,1)S(1)}, u32[]{:S(2)}, u32[]{:S(2)}) collective-permute-start(bf16[32,1152]{1,0:T(8,128)(2,1)S(1)} %get-tuple-element.44), channel_id=1, source_target_pairs={{0,8},{8,0},{16,24},{24,16},{1,9},{9,1},{17,25},{25,17},{2,10},{10... | collective-permute-start | bytes 221192 | tf_op jit(solution)/shard_map/ppermute | solution.py:341
  19.9 4.5 %collective-permute-start.4 = (bf16[32,1152]{1,0:T(8,128)(2,1)S(1)}, bf16[32,1152]{1,0:T(8,128)(2,1)S(1)}, u32[]{:S(2)}, u32[]{:S(2)}) collective-permute-start(bf16[32,1152]{1,0:T(8,128)(2,1)S(1)} %get-tuple-element.48), channel_id=1, source_target_pairs={{0,16},{8,24},{16,0},{24,8},{1,17},{9,25},{17,1},{25,9},{2,18},{10... | collective-permute-start | bytes 221192 | tf_op jit(solution)/shard_map/ppermute | solution.py:341
